TPU v7x, 32 devices: a whole 2x2x4 slice. The times are simulated.
32 devices in a mesh: freq: 4 (over z), tm: 2 (over core), beam: 4 (over y, x).
Axes of the slice: x: 2, y: 2, z: 4, core: 2. Of those that a mesh axis runs over, the one named last changes fastest.
Arguments:
- intensity: bfloat16 [4, 4096, 512], P('beam', 'freq', 'tm'), parts along dimension 0, may hold values from -32 to 32
- delay_tables: int32 [3, 12, 2048], replicated, may hold values from 0 to 511, as said below
- box_widths: int32 [8], replicated, may hold values from 1 to 128
Outputs:
- snr: float32 [4, 1024, 8, 512], P('beam', 'freq', None, 'tm'), parts along dimension 0
There are 4 independent parts, one for each index of `beam`. A program takes and returns all parts, laid end to end along the dimension named above; an argument that names none is the same for every part. Nothing has to cross between parts.
Inputs may be any that keep to these rules, and one draw needn't show every extreme that they name: `delay_tables`: at merge level s (second index s - 1), with D_s = max(1, 2^(s-2)), entry [k, s-1, b D_s + d] belongs to band b and trial d; the trials (k = 0, 1) and the delay (k = 2) lie in 0 to D_(s-1) - 1; columns from (4096 / 2^s) D_s on are not read.
All inputs are finite; a program needn't handle non-finite values.
Results may differ from a plain program's by a relative error of at most 0.0003.
Values may be sent and summed in bfloat16 or wider, within the bound.
A program may use at most 64 MiB of HBM per device.

v0:
```python
import jax
import jax.numpy as jnp
from jax import lax
from jax.sharding import PartitionSpec as P

LEVELS = 12
WMAX = 128


EPSILON = 1e-05

BANDS = ("freq", "tm")


def band_count():
    return lax.axis_size("freq") * lax.axis_size("tm")


def swapped(block, stride):
    count = band_count()
    route = []
    for low in range(count):
        high = low | 1 << stride
        if high != low and high < count:
            route += [(low, high), (high, low)]
    return lax.ppermute(block, BANDS, route)


def trial_depth(merge_level):
    if merge_level >= 2:
        return 2 ** (merge_level - 2)
    return 1


def shift_rows(source, delays, columns, largest):
    result = source
    for bit_index in range(max(largest, 0).bit_length()):
        step_size = 1 << bit_index
        moved = jnp.concatenate(
            [result[..., step_size:], jnp.zeros_like(result[..., :step_size])], axis=-1
        )
        flag = delays >> bit_index & 1 == 1
        result = jnp.where(flag[None, :, None], moved, result)
    return result[..., :columns]


def merge_bands(current, delay_tables, merge_level, first_band):
    beam_count, bands_in, depth_in, columns = current.shape
    depth_out = trial_depth(merge_level)
    bands_out = bands_in // 2
    entries = lax.dynamic_slice_in_dim(
        delay_tables[:, merge_level - 1, :], first_band * depth_out, bands_out * depth_out, 1
    )
    band_base = jnp.arange(bands_out * depth_out, dtype=jnp.int32) // depth_out * depth_in
    lower_flat = current[:, 0::2].reshape(beam_count, bands_out * depth_in, columns)
    upper_flat = current[:, 1::2].reshape(beam_count, bands_out * depth_in, columns)
    picked = jnp.take(lower_flat, band_base + entries[0], axis=1)
    chosen = jnp.take(upper_flat, band_base + entries[1], axis=1)
    delayed = shift_rows(chosen, entries[2], columns, depth_in - 1)
    return (picked + delayed).reshape(beam_count, bands_out, depth_out, columns)


def merge_across(current, delay_tables, merge_level, cross_step, device_pos):
    beam_count, rows_held, columns = current.shape
    depth_in = rows_held * 2**cross_step
    depth_out = trial_depth(merge_level)
    group_size = 2 ** (cross_step + 1)
    position = device_pos % group_size
    upper_side = position // (group_size // 2)
    row_offset = position % (group_size // 2) * rows_held
    band_index = device_pos // group_size
    entries = lax.dynamic_slice_in_dim(
        delay_tables[:, merge_level - 1, :], band_index * depth_out, depth_out, 1
    )
    lower_local = entries[0] - row_offset
    lower_hit = (lower_local >= 0) & (lower_local < rows_held) & (upper_side == 0)
    lower_rows = jnp.take(current, jnp.clip(lower_local, 0, rows_held - 1), axis=1)
    upper_local = entries[1] - row_offset
    upper_hit = (upper_local >= 0) & (upper_local < rows_held) & (upper_side == 1)
    upper_chosen = jnp.take(current, jnp.clip(upper_local, 0, rows_held - 1), axis=1)
    upper_rows = shift_rows(upper_chosen, entries[2], columns, depth_in - 1)
    partial_value = jnp.where(lower_hit[None, :, None], lower_rows, 0.0) + jnp.where(
        upper_hit[None, :, None], upper_rows, 0.0
    )
    for bit_index in range(cross_step + 1):
        blocks = partial_value.shape[1] // rows_held
        paired = partial_value.reshape(beam_count, blocks // 2, 2, rows_held, columns)
        chosen_bit = device_pos >> bit_index & 1
        kept_rows = lax.dynamic_index_in_dim(paired, chosen_bit, 2, keepdims=False)
        given_rows = lax.dynamic_index_in_dim(paired, 1 - chosen_bit, 2, keepdims=False)
        partial_value = (kept_rows + swapped(given_rows, bit_index)).reshape(
            beam_count, blocks // 2 * rows_held, columns
        )
    return partial_value


def body(intensity, delay_tables, box_widths):
    time_parts = lax.axis_size("tm")
    time_pos = lax.axis_index("tm")
    device_pos = lax.axis_index("freq") * time_parts + time_pos
    block_len = intensity.shape[2]
    whole_rows = lax.all_to_all(intensity, "tm", 1, 2, tiled=True)
    beam_count, channels_held, time_total = whole_rows.shape
    local_levels = channels_held.bit_length() - 1
    current = whole_rows.astype(jnp.float32)[:, :, None, :]
    for merge_level in range(1, local_levels + 1):
        current = merge_bands(
            current, delay_tables, merge_level, device_pos * (channels_held >> merge_level)
        )
    dedispersed = current[:, 0]
    for cross_step in range(LEVELS - local_levels):
        dedispersed = merge_across(
            dedispersed, delay_tables, local_levels + cross_step + 1, cross_step, device_pos
        )
    average = jnp.sum(dedispersed, axis=-1) / time_total
    deviation = dedispersed - average[..., None]
    spread = jnp.sum(deviation * deviation, axis=-1) / time_total
    inverse = lax.rsqrt(spread + EPSILON)
    scaled = deviation * inverse[..., None]
    scaled = lax.all_gather(scaled, "tm", axis=1, tiled=True)
    padded = jnp.pad(scaled, ((0, 0), (0, 0), (0, WMAX)))
    window = lax.dynamic_slice_in_dim(padded, time_pos * block_len, block_len + WMAX, 2)
    running = jnp.cumsum(jnp.pad(window, ((0, 0), (0, 0), (1, 0))), axis=-1)
    leading_sum = running[..., :block_len]
    filtered = []
    for width_index in range(box_widths.shape[0]):
        ending = lax.dynamic_slice_in_dim(running, box_widths[width_index], block_len, 2)
        filtered.append(ending - leading_sum)
    boxed = jnp.stack(filtered, axis=2)
    return boxed * lax.rsqrt(box_widths.astype(jnp.float32))[None, None, :, None]


def solution(mesh):
    in_specs = (P("beam", "freq", "tm"), P(), P())
    out_specs = P("beam", "freq", None, "tm")
    return jax.shard_map(body, mesh=mesh, in_specs=in_specs, out_specs=out_specs, check_vma=False)
```

profile of v0, /device:TPU:0, one launch (start us, length us, event | category | flops | bytes accessed | tf_op | source)
XLA Modules:
  0.0 127.5 jit_solution(16081477878346063945)
XLA Ops:
  0.0 1.9 %copy.39 = bf16[1,1024,256]{2,0,1:T(2,128)(2,1)S(1)} copy(bf16[1,1024,256]{2,1,0:T(8,128)(2,1)} %param.15) | data formatting | bytes 1048576 | tf_op args[0]
  2.4 3.8 %reduce.63 = bf16[1024,256]{1,0:T(8,128)(2,1)S(1)} reduce(bf16[1024,1,256]{2,1,0:T(2,128)(2,1)S(1)} %bitcast.423, bf16[]{:T(256)} %broadcast.1530), dimensions={1}, to_apply=%bitcast.406.reduce_sub_computation | reduce | bytes 1048578
  6.2 0.9 reshape.1898
  7.1 3.5 %all-to-all-start = ((bf16[2,2,65536]{2,1,0:T(2,128)(2,1)}), bf16[2,2,65536]{2,1,0:T(2,128)(2,1)S(1)}, u32[]{:S(2)}, u32[]{:S(2)}) async-start(bf16[2,2,65536]{2,1,0:T(2,128)(2,1)} %reshape.1898), calls=%async_computation | async-start | bytes 1048576 | tf_op jit(solution)/shard_map/all_to_all | solution.py:102
  10.6 1.7 %all-to-all-done = bf16[2,2,65536]{2,1,0:T(2,128)(2,1)S(1)} async-done(((bf16[2,2,65536]{2,1,0:T(2,128)(2,1)}), bf16[2,2,65536]{2,1,0:T(2,128)(2,1)S(1)}, u32[]{:S(2)}, u32[]{:S(2)}) %all-to-all-start) | async-done | bytes 524320 | tf_op jit(solution)/shard_map/all_to_all | solution.py:102
  12.8 0.8 copy.38
  13.6 0.8 reshape.1502
  15.6 0.8 fusion.70
  16.5 1.0 gather_fusion
  17.4 1.0 gather_fusion.1
  19.3 0.8 gather_fusion.2
  20.0 0.8 gather_fusion.3
  21.6 0.8 gather_fusion.4
  22.3 0.8 gather_fusion.5
  23.5 0.8 gather_fusion.7
  24.6 0.8 gather_fusion.6
  25.7 0.8 gather_fusion.9
  27.0 0.8 gather_fusion.8
  27.9 0.8 gather_fusion.11
  29.4 0.8 gather_fusion.10
  30.3 0.8 gather_fusion.13
  32.0 0.8 gather_fusion.12
  32.9 0.8 gather_fusion.15
  34.9 0.8 gather_fusion.14
  35.8 0.8 gather_fusion.17
  38.0 0.8 gather_fusion.16
  38.9 1.0 gather_fusion.19
  42.2 1.0 gather_fusion.18
  43.8 1.2 collective-permute-done
  45.1 1.8 %gather_fusion.21 = f32[512,512]{1,0:T(8,128)S(1)} fusion(f32[128,512]{1,0:T(8,128)S(1)} %fusion.10, s32[1024]{0:T(1024)S(1)} %pad_clamp_fusion), kind=kCustom, calls=%fused_computation.22.clone | custom fusion | bytes 2099200 | tf_op jit(solution)/shard_map/jit(_take)/gather | solution.py:80
  50.7 0.9 slice.601
  51.7 1.6 %gather_fusion.20 = f32[512,512]{1,0:T(8,128)S(1)} fusion(f32[128,512]{1,0:T(8,128)S(1)} %fusion.10, s32[1024]{0:T(1024)S(1)} %pad_clamp_fusion.1), kind=kCustom, calls=%fused_computation.4.clone | custom fusion | bytes 2099200 | tf_op jit(solution)/shard_map/jit(_take)/gather | solution.py:77
  53.3 1.6 %fusion.3 = f32[1,512,512]{2,1,0:T(8,128)S(1)} fusion(f32[512,512]{1,0:T(8,128)S(1)} %gather_fusion.20, f32[1,512,512]{2,1,0:T(8,128)S(1)} %pad_select_fusion.8, f32[1,512,384]{2,1,0:T(8,128)} %slice.601, pred[512]{0:T(512)(128)(4,1)S(1)} %get-tuple-element.190, pred[512]{0:T(512)(128)(4,1)S(1)} %get-tuple-element.26, ...), kind=kLoop, calls=%fused_computation.40 | loop fusion | flops 1310720 | bytes 3934208 | tf_op jit(solution)/shard_map/add | solution.py:82
  55.2 1.8 %collective-permute-done.1 = f32[1,2,128,512]{3,2,1,0:T(8,128)S(1)} collective-permute-done((f32[1,2,128,512]{3,2,1,0:T(8,128)S(1)}, f32[1,2,128,512]{3,2,1,0:T(8,128)S(1)}, u32[]{:S(2)}, u32[]{:S(2)}) %collective-permute-start.1) | collective-permute-done | bytes 524320 | tf_op jit(solution)/shard_map/ppermute | solution.py:26
  57.0 3.1 %collective-permute-start.2 = (f32[1,1,128,512]{3,2,1,0:T(8,128)S(1)}, f32[1,1,128,512]{3,2,1,0:T(8,128)S(1)}, u32[]{:S(2)}, u32[]{:S(2)}) collective-permute-start(f32[1,1,128,512]{3,2,1,0:T(8,128)S(1)} %constant_dynamic-slice_fusion.22), channel_id=1, source_target_pairs={{0,8},{8,0},{4,12},{12,4},{16,24},{24,16},{20,28},{28,20},{1,9},{9... | collective-permute-start | bytes 786440 | tf_op jit(solution)/shard_map/ppermute | solution.py:26
  60.4 6.4 %collective-permute-done.2 = f32[1,1,128,512]{3,2,1,0:T(8,128)S(1)} collective-permute-done((f32[1,1,128,512]{3,2,1,0:T(8,128)S(1)}, f32[1,1,128,512]{3,2,1,0:T(8,128)S(1)}, u32[]{:S(2)}, u32[]{:S(2)}) %collective-permute-start.2) | collective-permute-done | bytes 262176 | tf_op jit(solution)/shard_map/ppermute | solution.py:26
  66.8 3.5 %gather_fusion.23 = f32[1024,512]{1,0:T(8,128)S(1)} fusion(f32[128,512]{1,0:T(8,128)S(1)} %add_bitcast_fusion, s32[1024]{0:T(1024)S(1)} %get-tuple-element.188), kind=kCustom, calls=%fused_computation.23.clone | custom fusion | bytes 4198400 | tf_op jit(solution)/shard_map/jit(_take)/gather | solution.py:80
  70.6 0.6 slice.602
  71.2 1.0 pad_select_fusion.7
  78.0 4.9 %gather_fusion.22 = f32[1024,512]{1,0:T(8,128)} fusion(f32[128,512]{1,0:T(8,128)S(1)} %add_bitcast_fusion, s32[1024]{0:T(1024)S(1)} %get-tuple-element.187), kind=kCustom, calls=%fused_computation.5.clone | custom fusion | bytes 4198400 | tf_op jit(solution)/shard_map/jit(_take)/gather | solution.py:77
  82.9 2.9 %fusion.1 = f32[1,1024,512]{2,1,0:T(8,128)S(1)} fusion(f32[1024,512]{1,0:T(8,128)} %gather_fusion.22, f32[1,1024,512]{2,1,0:T(8,128)S(1)} %pad_select_fusion, f32[1,1024,256]{2,1,0:T(8,128)S(1)} %slice.610, pred[1024]{0:T(1024)(128)(4,1)S(1)} %get-tuple-element.186, pred[1024]{0:T(1024)(128)(4,1)S(1)} %get-tuple-element.20, ...), kind=kLoop, calls=%fused_computation.27 | loop fusion | flops 2621440 | bytes 7344128 | tf_op jit(solution)/shard_map/add | solution.py:82
  86.0 2.6 %collective-permute-done.3 = f32[1,4,128,512]{3,2,1,0:T(8,128)S(1)} collective-permute-done((f32[1,4,128,512]{3,2,1,0:T(8,128)S(1)}, f32[1,4,128,512]{3,2,1,0:T(8,128)S(1)}, u32[]{:S(2)}, u32[]{:S(2)}) %collective-permute-start.3) | collective-permute-done | bytes 1048608 | tf_op jit(solution)/shard_map/ppermute | solution.py:26
  88.9 1.8 %collective-permute-start.4 = (f32[1,2,128,512]{3,2,1,0:T(8,128)S(1)}, f32[1,2,128,512]{3,2,1,0:T(8,128)S(1)}, u32[]{:S(2)}, u32[]{:S(2)}) collective-permute-start(f32[1,2,128,512]{3,2,1,0:T(8,128)S(1)} %dynamic-slice_bitcast_fusion.1), channel_id=1, source_target_pairs={{0,8},{8,0},{4,12},{12,4},{16,24},{24,16},{20,28},{28,20},{1,9},{9... | collective-permute-start | bytes 1572872 | tf_op jit(solution)/shard_map/ppermute | solution.py:26
  90.7 12.2 %collective-permute-done.4 = f32[1,2,128,512]{3,2,1,0:T(8,128)S(1)} collective-permute-done((f32[1,2,128,512]{3,2,1,0:T(8,128)S(1)}, f32[1,2,128,512]{3,2,1,0:T(8,128)S(1)}, u32[]{:S(2)}, u32[]{:S(2)}) %collective-permute-start.4) | collective-permute-done | bytes 524320 | tf_op jit(solution)/shard_map/ppermute | solution.py:26
  103.1 2.8 %collective-permute-start.5 = (f32[1,1,128,512]{3,2,1,0:T(8,128)S(1)}, f32[1,1,128,512]{3,2,1,0:T(8,128)S(1)}, u32[]{:S(2)}, u32[]{:S(2)}) collective-permute-start(f32[1,1,128,512]{3,2,1,0:T(8,128)S(1)} %constant_dynamic-slice_fusion.21), channel_id=1, source_target_pairs={{0,16},{16,0},{4,20},{20,4},{8,24},{24,8},{12,28},{28,12},{1,17},{... | collective-permute-start | bytes 786440 | tf_op jit(solution)/shard_map/ppermute | solution.py:26
  105.9 0.7 fusion.75
  121.9 2.2 %all_gather.3 = f32[1,256,512]{2,1,0:T(8,128)S(1)} all-gather(f32[1,128,512]{2,1,0:T(8,128)S(1)} %fusion.22), channel_id=1, replica_groups=mesh['freq'=4,'tm'=2,'beam'=4] {'tm'}, dimensions={1}, use_global_device_ids=true | all-gather | bytes 786432 | tf_op jit(solution)/shard_map/all_gather | solution.py:120
  125.6 2.0 %copy.31 = f32[1,256,8,256]{3,2,1,0:T(8,128)} copy(f32[1,256,8,256]{1,3,2,0:T(8,128)S(1)} %broadcast_multiply_fusion) | data formatting | bytes 4194304 | tf_op jit(solution)/shard_map/mul | solution.py:130
  (215 shorter events, 25.2 us)
Async XLA Ops:
  7.1 5.2 %all-to-all-start = ((bf16[2,2,65536]{2,1,0:T(2,128)(2,1)}), bf16[2,2,65536]{2,1,0:T(2,128)(2,1)S(1)}, u32[]{:S(2)}, u32[]{:S(2)}) async-start(bf16[2,2,65536]{2,1,0:T(2,128)(2,1)} %reshape.1898), calls=%async_computation | async-start | bytes 1048576 | tf_op jit(solution)/shard_map/all_to_all | solution.py:102
  13.6 2.0 %copy-start = (s32[3,12,2048]{2,1,0:T(8,128)S(1)}, s32[3,12,2048]{2,1,0:T(8,128)}, u32[]{:S(2)}) copy-start(s32[3,12,2048]{2,1,0:T(8,128)} %param.16) | copy-start | bytes 884740
  43.5 1.6 %collective-permute-start = (f32[1,1,128,512]{3,2,1,0:T(8,128)S(1)}, f32[1,1,128,512]{3,2,1,0:T(8,128)S(1)}, u32[]{:S(2)}, u32[]{:S(2)}) collective-permute-start(f32[1,1,128,512]{3,2,1,0:T(8,128)S(1)} %dynamic-slice_bitcast_fusion.3), channel_id=1, source_target_pairs={{0,4},{4,0},{8,12},{12,8},{16,20},{20,16},{24,28},{28,24},{1,5},{5... | collective-permute-start | bytes 786440 | tf_op jit(solution)/shard_map/ppermute | solution.py:26
  53.3 1.8 %copy-start.1 = (s32[3,1,2048]{2,1,0:T(1,128)S(1)}, s32[3,1,2048]{2,1,0:T(1,128)}, u32[]{:S(2)}) copy-start(s32[3,1,2048]{2,1,0:T(1,128)} %get-tuple-element.83) | copy-start | bytes 73732
  54.9 2.0 %collective-permute-start.1 = (f32[1,2,128,512]{3,2,1,0:T(8,128)S(1)}, f32[1,2,128,512]{3,2,1,0:T(8,128)S(1)}, u32[]{:S(2)}, u32[]{:S(2)}) collective-permute-start(f32[1,2,128,512]{3,2,1,0:T(8,128)S(1)} %dynamic-slice_bitcast_fusion.2), channel_id=1, source_target_pairs={{0,4},{4,0},{8,12},{12,8},{16,20},{20,16},{24,28},{28,24},{1,5},{5... | collective-permute-start | bytes 1572872 | tf_op jit(solution)/shard_map/ppermute | solution.py:26
  57.0 9.7 %collective-permute-start.2 = (f32[1,1,128,512]{3,2,1,0:T(8,128)S(1)}, f32[1,1,128,512]{3,2,1,0:T(8,128)S(1)}, u32[]{:S(2)}, u32[]{:S(2)}) collective-permute-start(f32[1,1,128,512]{3,2,1,0:T(8,128)S(1)} %constant_dynamic-slice_fusion.22), channel_id=1, source_target_pairs={{0,8},{8,0},{4,12},{12,4},{16,24},{24,16},{20,28},{28,20},{1,9},{9... | collective-permute-start | bytes 786440 | tf_op jit(solution)/shard_map/ppermute | solution.py:26
  85.9 2.7 %collective-permute-start.3 = (f32[1,4,128,512]{3,2,1,0:T(8,128)S(1)}, f32[1,4,128,512]{3,2,1,0:T(8,128)S(1)}, u32[]{:S(2)}, u32[]{:S(2)}) collective-permute-start(f32[1,4,128,512]{3,2,1,0:T(8,128)S(1)} %dynamic-slice_bitcast_fusion), channel_id=1, source_target_pairs={{0,4},{4,0},{8,12},{12,8},{16,20},{20,16},{24,28},{28,24},{1,5},{5... | collective-permute-start | bytes 3145736 | tf_op jit(solution)/shard_map/ppermute | solution.py:26
  88.8 17.0 %copy-start.2 = (s32[8]{0:T(128)S(1)}, s32[8]{0:T(128)}, u32[]{:S(2)}) copy-start(s32[8]{0:T(128)} %param.17) | copy-start | bytes 100
  88.9 14.0 %collective-permute-start.4 = (f32[1,2,128,512]{3,2,1,0:T(8,128)S(1)}, f32[1,2,128,512]{3,2,1,0:T(8,128)S(1)}, u32[]{:S(2)}, u32[]{:S(2)}) collective-permute-start(f32[1,2,128,512]{3,2,1,0:T(8,128)S(1)} %dynamic-slice_bitcast_fusion.1), channel_id=1, source_target_pairs={{0,8},{8,0},{4,12},{12,4},{16,24},{24,16},{20,28},{28,20},{1,9},{9... | collective-permute-start | bytes 1572872 | tf_op jit(solution)/shard_map/ppermute | solution.py:26
  103.1 18.3 %collective-permute-start.5 = (f32[1,1,128,512]{3,2,1,0:T(8,128)S(1)}, f32[1,1,128,512]{3,2,1,0:T(8,128)S(1)}, u32[]{:S(2)}, u32[]{:S(2)}) collective-permute-start(f32[1,1,128,512]{3,2,1,0:T(8,128)S(1)} %constant_dynamic-slice_fusion.21), channel_id=1, source_target_pairs={{0,16},{16,0},{4,20},{20,4},{8,24},{24,8},{12,28},{28,12},{1,17},{... | collective-permute-start | bytes 786440 | tf_op jit(solution)/shard_map/ppermute | solution.py:26
where the time goes:
time: 128 us
  local copies, waits for them, and re-layouts  51.8 us (40%)
  waiting for transfers between devices  26 us (20%)
  other arithmetic  19.4 us (15%)
  between operations  16.5 us (13%)
  starting transfers between devices  11.7 us (9%)
  blocking collectives  2.18 us (2%)
    ppermute x6, waiting for transfers between devices, swapped(): return lax.ppermute(block, BANDS, route)  24.2 us
    slice x45, local copies, waits for them, and re-layouts, shift_rows(): result[..., step_size:]  11.8 us
    ppermute x6, starting transfers between devices, swapped(): return lax.ppermute(block, BANDS, route)  8.21 us
    gather x3, local copies, waits for them, and re-layouts, merge_across(): jnp.take(current, jnp.clip(lower_local, 0, rows_held - 1), axis=1)  7.46 us
    gather x9, local copies, waits for them, and re-layouts, merge_bands(): chosen = jnp.take(upper_flat, band_base + entries[1], axis=1)  7.02 us
    gather x9, local copies, waits for them, and re-layouts, merge_bands(): picked = jnp.take(lower_flat, band_base + entries[0], axis=1)  7.02 us
    select_n x36, other arithmetic, shift_rows(): result = jnp.where(flag[None, :, None], moved, result)  6.33 us
    gather x3, local copies, waits for them, and re-layouts, merge_across(): jnp.take(current, jnp.clip(upper_local, 0, rows_held - 1), axis=1)  6.32 us
  transfers between devices with their start and end apart: 7, of which 6 were waited for; matrix products, arithmetic and copies ran while one was open for 1% of the time, Pallas kernels for 0%

commit v1 on v0

--- a/solution.py
+++ b/solution.py
@@ -94,6 +94,16 @@
     return partial_value
 
 
+def own_trials(current, delay_tables, device_pos):
+    beam_count, bands_in, depth_in, columns = current.shape
+    rows = trial_depth(LEVELS) // band_count()
+    entries = lax.dynamic_slice_in_dim(delay_tables[:, LEVELS - 1, :], device_pos * rows, rows, 1)
+    picked = jnp.take(current[:, 0], entries[0], axis=1)
+    chosen = jnp.take(current[:, 1], entries[1], axis=1)
+    delayed = shift_rows(chosen, entries[2], columns, depth_in - 1)
+    return picked + delayed
+
+
 def body(intensity, delay_tables, box_widths):
     time_parts = lax.axis_size("tm")
     time_pos = lax.axis_index("tm")
@@ -107,11 +117,14 @@
         current = merge_bands(
             current, delay_tables, merge_level, device_pos * (channels_held >> merge_level)
         )
-    dedispersed = current[:, 0]
-    for cross_step in range(LEVELS - local_levels):
-        dedispersed = merge_across(
-            dedispersed, delay_tables, local_levels + cross_step + 1, cross_step, device_pos
-        )
+    merged_levels = local_levels
+    if merged_levels < LEVELS:
+        current = lax.all_gather(current, BANDS, axis=1, tiled=True)
+        for merge_level in range(merged_levels + 1, LEVELS):
+            current = merge_bands(current, delay_tables, merge_level, 0)
+        dedispersed = own_trials(current, delay_tables, device_pos)
+    else:
+        dedispersed = current[:, 0]
     average = jnp.sum(dedispersed, axis=-1) / time_total
     deviation = dedispersed - average[..., None]
     spread = jnp.sum(deviation * deviation, axis=-1) / time_total

time: 128 us -> 144 us (1.12)
  local copies, waits for them, and re-layouts: 51.8 us -> 65.7 us
  between operations: 16.5 us -> 29.5 us
  starting transfers between devices: 11.7 us -> 3.53 us
  waiting for transfers between devices: 26 us -> 18 us
  other arithmetic: 19.4 us -> 24.3 us
    ppermute x6 -> x0, waiting for transfers between devices: 24.2 us -> none  [swapped(): return lax.ppermute(block, BANDS, route)]
    all_gather x0 -> x1, waiting for transfers between devices: none -> 16.3 us  [body(): current = lax.all_gather(current, BANDS, axis=1, tiled=True)]
    gather x6 -> x2, local copies, waits for them, and re-layouts: 13.8 us -> 1.51 us  [the longest x1 0.76 us: own_trials(): chosen = jnp.take(current[:, 1], entries[1], axis=1)]
    gather x9 -> x11, local copies, waits for them, and re-layouts: 7.02 us -> 16.8 us  [merge_bands(): chosen = jnp.take(upper_flat, band_base + entries[1], axis=1)]
    gather x9 -> x11, local copies, waits for them, and re-layouts: 7.02 us -> 16.8 us  [merge_bands(): picked = jnp.take(lower_flat, band_base + entries[0], axis=1)]
    ppermute x6 -> x0, starting transfers between devices: 8.21 us -> none  [swapped(): return lax.ppermute(block, BANDS, route)]
    add x5 -> x8, other arithmetic: 0.53 us -> 6.29 us  [merge_bands(): return (picked + delayed).reshape(beam_count, bands_out, depth_out, columns)]
    add x6 -> x0, other arithmetic: 5.05 us -> none  [the longest x3 4.68 us: merge_across(): jnp.where(lower_hit[None, :, None], lower_rows, 0.0)]
  transfers between devices with their start and end apart: 7 -> 2, of which waited for: 6 -> 2; matrix products, arithmetic and copies ran while one was open for 1% -> 1% of each run, Pallas kernels for 0% -> 0%
where the time goes in v1:
time: 144 us; the launch traced here: 143 us
  local copies, waits for them, and re-layouts  65.7 us (46%)
  between operations  29.5 us (20%)
  other arithmetic  24.3 us (17%)
  waiting for transfers between devices  18 us (12%)
  starting transfers between devices  3.53 us (2%)
  blocking collectives  2.18 us (2%)
    gather x11, local copies, waits for them, and re-layouts, merge_bands(): chosen = jnp.take(upper_flat, band_base + entries[1], axis=1)  16.8 us
    gather x11, local copies, waits for them, and re-layouts, merge_bands(): picked = jnp.take(lower_flat, band_base + entries[0], axis=1)  16.8 us
    all_gather x1, waiting for transfers between devices, body(): current = lax.all_gather(current, BANDS, axis=1, tiled=True)  16.3 us
    slice x45, local copies, waits for them, and re-layouts, shift_rows(): result[..., step_size:]  14.7 us
    select_n x36, other arithmetic, shift_rows(): result = jnp.where(flag[None, :, None], moved, result)  7.66 us
    add x8, other arithmetic, merge_bands(): return (picked + delayed).reshape(beam_count, bands_out, depth_out, columns)  6.29 us
    unnamed x12, local copies, waits for them, and re-layouts  5.69 us
    unnamed x8, other arithmetic  4.15 us
  transfers between devices with their start and end apart: 2, of which 2 were waited for; matrix products, arithmetic and copies ran while one was open for 1% of the time, Pallas kernels for 0%

profile of v1, /device:TPU:0, one launch (start us, length us, event | category | flops | bytes accessed | tf_op | source)
XLA Modules:
  0.0 143.2 jit_solution(5230237503584928580)
XLA Ops:
  6.5 1.9 %copy.33 = bf16[1,1024,256]{2,0,1:T(2,128)(2,1)S(1)} copy(bf16[1,1024,256]{2,1,0:T(8,128)(2,1)} %param.13) | data formatting | bytes 1048576 | tf_op args[0]
  8.9 3.8 %reduce.32 = bf16[1024,256]{1,0:T(8,128)(2,1)S(1)} reduce(bf16[1024,1,256]{2,1,0:T(2,128)(2,1)S(1)} %bitcast.431, bf16[]{:T(256)} %broadcast.1330), dimensions={1}, to_apply=%bitcast.414.reduce_sub_computation | reduce | bytes 1048578
  12.7 0.9 reshape.1617
  13.6 3.5 %all-to-all-start = ((bf16[2,2,65536]{2,1,0:T(2,128)(2,1)}), bf16[2,2,65536]{2,1,0:T(2,128)(2,1)S(1)}, u32[]{:S(2)}, u32[]{:S(2)}) async-start(bf16[2,2,65536]{2,1,0:T(2,128)(2,1)} %reshape.1617), calls=%async_computation | async-start | bytes 1048576 | tf_op jit(solution)/shard_map/all_to_all | solution.py:112
  17.2 1.7 %all-to-all-done = bf16[2,2,65536]{2,1,0:T(2,128)(2,1)S(1)} async-done(((bf16[2,2,65536]{2,1,0:T(2,128)(2,1)}), bf16[2,2,65536]{2,1,0:T(2,128)(2,1)S(1)}, u32[]{:S(2)}, u32[]{:S(2)}) %all-to-all-start) | async-done | bytes 524320 | tf_op jit(solution)/shard_map/all_to_all | solution.py:112
  19.3 0.8 copy.32
  20.2 0.8 reshape.1235
  22.4 1.0 gather_fusion
  23.4 1.0 gather_fusion.1
  25.2 0.8 gather_fusion.2
  26.0 0.8 gather_fusion.3
  27.5 0.8 gather_fusion.4
  28.2 0.8 gather_fusion.5
  29.4 0.8 gather_fusion.7
  30.5 0.8 gather_fusion.6
  31.6 0.8 gather_fusion.9
  32.9 0.8 gather_fusion.8
  33.8 0.8 gather_fusion.11
  35.3 0.8 gather_fusion.10
  36.2 0.8 gather_fusion.13
  37.9 0.8 gather_fusion.12
  38.9 0.8 gather_fusion.15
  40.8 0.8 gather_fusion.14
  41.7 0.8 gather_fusion.17
  44.0 0.8 gather_fusion.16
  44.7 0.8 fusion.5
  45.6 0.7 fusion.79
  61.3 16.3 %all-gather.3.cloned.1.call-done = f32[8,128,512]{2,1,0:T(8,128)} async-done(((f32[1,128,512]{2,1,0:T(8,128)}), f32[8,128,512]{2,1,0:T(8,128)}) %all-gather.3.cloned.1.call-update) | async-done | bytes 2097168 | tf_op jit(solution)/shard_map/all_gather | solution.py:122
  77.6 1.8 %fusion.71 = (f32[1,4,128,512]{3,2,1,0:T(8,128)S(1)}, f32[1,4,128,512]{3,2,1,0:T(8,128)S(1)}) fusion(f32[1,8,128,512]{3,2,1,0:T(8,128)} %bitcast.434), kind=kLoop, calls=%fused_computation.354 | loop fusion | bytes 4194304 | tf_op jit(solution)/shard_map/slice | solution.py:56
  79.4 4.9 %gather_fusion.19 = f32[1024,512]{1,0:T(8,128)} fusion(f32[512,512]{1,0:T(8,128)S(1)} %bitcast.417, s32[1024]{0:T(1024)S(1)} %broadcast_clamp_fusion.2), kind=kCustom, calls=%fused_computation.20.clone | custom fusion | bytes 4198400 | tf_op jit(solution)/shard_map/jit(_take)/gather | solution.py:58
  84.3 1.8 %bitcast_select_fusion.2 = f32[1,1024,512]{2,1,0:T(8,128)S(1)} fusion(f32[1024,512]{1,0:T(8,128)} %gather_fusion.19, pred[1024]{0:T(1024)(128)(4,1)S(1)} %compare_and_fusion.2), kind=kLoop, calls=%fused_computation.27 | loop fusion | flops 524288 | bytes 4195328 | tf_op jit(solution)/shard_map/jit(_take)/select_n | solution.py:58
  86.1 0.6 slice.615
  86.7 1.0 copy-done
  87.7 1.2 pad_select_fusion.12
  93.3 2.0 %slice.621 = f32[1,1024,448]{2,1,0:T(8,128)} slice(f32[1,1024,512]{2,1,0:T(8,128)S(1)} %pad_select_fusion.7), slice={[0:1], [0:1024], [64:512]} | slice | bytes 3670016 | tf_op jit(solution)/shard_map/slice | solution.py:40
  95.3 4.9 %gather_fusion.18 = f32[1024,512]{1,0:T(8,128)} fusion(f32[512,512]{1,0:T(8,128)S(1)} %bitcast.416, s32[1024]{0:T(1024)S(1)} %broadcast_clamp_fusion.3), kind=kCustom, calls=%fused_computation.3.clone | custom fusion | bytes 4198400 | tf_op jit(solution)/shard_map/jit(_take)/gather | solution.py:57
  100.2 2.6 %fusion.1 = f32[1,1024,512]{2,1,0:T(8,128)S(1)} fusion(f32[1024,512]{1,0:T(8,128)} %gather_fusion.18, f32[1,1024,512]{2,1,0:T(8,128)S(1)} %pad_select_fusion.7, f32[1,1024,448]{2,1,0:T(8,128)} %slice.621, pred[1024]{0:T(1024)(128)(4,1)S(1)} %compare_and_fusion.3, pred[1024]{0:T(1024)(128)(4,1)S(1)} %get-tuple-element.18), kind=kLoop, calls=%fused_computation.29 | loop fusion | flops 1572864 | bytes 8128512 | tf_op jit(solution)/shard_map/add | solution.py:60
  102.9 4.9 %gather_fusion.21 = f32[1024,512]{1,0:T(8,128)} fusion(f32[512,512]{1,0:T(8,128)S(1)} %bitcast.418, s32[1024]{0:T(1024)S(1)} %broadcast_clamp_fusion), kind=kCustom, calls=%fused_computation.22.clone | custom fusion | bytes 4198400 | tf_op jit(solution)/shard_map/jit(_take)/gather | solution.py:58
  107.8 1.8 %bitcast_select_fusion = f32[1,1024,512]{2,1,0:T(8,128)S(1)} fusion(f32[1024,512]{1,0:T(8,128)} %gather_fusion.21, pred[1024]{0:T(1024)(128)(4,1)S(1)} %compare_and_fusion), kind=kLoop, calls=%fused_computation.24 | loop fusion | flops 524288 | bytes 4195328 | tf_op jit(solution)/shard_map/jit(_take)/select_n | solution.py:58
  110.2 1.0 copy-done.1
  111.2 1.3 pad_select_fusion.6
  117.8 1.3 slice.631
  119.1 4.9 %gather_fusion.20 = f32[1024,512]{1,0:T(8,128)} fusion(f32[512,512]{1,0:T(8,128)S(1)} %bitcast.415, s32[1024]{0:T(1024)S(1)} %broadcast_clamp_fusion.1), kind=kCustom, calls=%fused_computation.21.clone | custom fusion | bytes 4198400 | tf_op jit(solution)/shard_map/jit(_take)/gather | solution.py:57
  123.9 2.4 %fusion = f32[1,1024,512]{2,1,0:T(8,128)S(1)} fusion(f32[1024,512]{1,0:T(8,128)} %gather_fusion.20, f32[1,1024,512]{2,1,0:T(8,128)S(1)} %pad_select_fusion, f32[1,1024,384]{2,1,0:T(8,128)} %slice.631, pred[1024]{0:T(1024)(128)(4,1)S(1)} %compare_and_fusion.1, pred[1024]{0:T(1024)(128)(4,1)S(1)} %get-tuple-element.6), kind=kLoop, calls=%fused_computation.26 | loop fusion | flops 1572864 | bytes 7866368 | tf_op jit(solution)/shard_map/add | solution.py:60
  126.5 0.8 gather_fusion.23
  129.2 0.8 gather_fusion.22
  130.4 2.2 %all_gather.7 = f32[1,256,512]{2,1,0:T(8,128)S(1)} all-gather(f32[1,128,512]{2,1,0:T(8,128)S(1)} %subtract_multiply_fusion), channel_id=1, replica_groups=mesh['freq'=4,'tm'=2,'beam'=4] {'tm'}, dimensions={1}, use_global_device_ids=true | all-gather | bytes 786432 | tf_op jit(solution)/shard_map/all_gather | solution.py:133
  134.4 2.0 %copy.25 = f32[1,256,8,256]{3,2,1,0:T(8,128)} copy(f32[1,256,8,256]{1,3,2,0:T(8,128)S(1)} %broadcast_multiply_fusion) | data formatting | bytes 4194304 | tf_op jit(solution)/shard_map/mul | solution.py:143
  (197 shorter events, 24.7 us)
Async XLA Ops:
  13.6 5.2 %all-to-all-start = ((bf16[2,2,65536]{2,1,0:T(2,128)(2,1)}), bf16[2,2,65536]{2,1,0:T(2,128)(2,1)S(1)}, u32[]{:S(2)}, u32[]{:S(2)}) async-start(bf16[2,2,65536]{2,1,0:T(2,128)(2,1)} %reshape.1617), calls=%async_computation | async-start | bytes 1048576 | tf_op jit(solution)/shard_map/all_to_all | solution.py:112
  17.1 60.5 %all-gather.3.cloned.1.call-start = ((), (), s32[]{:S(2)}) async-start(), calls=%async_computation.1 | async-start | bytes 2359296 | tf_op jit(solution)/shard_map/all_gather | solution.py:122
  20.1 2.0 %copy-start.2 = (s32[3,12,2048]{2,1,0:T(8,128)S(1)}, s32[3,12,2048]{2,1,0:T(8,128)}, u32[]{:S(2)}) copy-start(s32[3,12,2048]{2,1,0:T(8,128)} %param.14) | copy-start | bytes 884740
  43.8 1.8 %copy-start.3 = (s32[8]{0:T(128)S(1)}, s32[8]{0:T(128)}, u32[]{:S(2)}) copy-start(s32[8]{0:T(128)} %param.15) | copy-start | bytes 100
  86.1 1.6 %copy-start = (f32[1024,512]{1,0:T(8,128)S(1)}, f32[1024,512]{1,0:T(8,128)}, u32[]{:S(2)}) copy-start(f32[1024,512]{1,0:T(8,128)} %gather_fusion.19) | copy-start | bytes 6291460
  109.6 1.6 %copy-start.1 = (f32[1024,512]{1,0:T(8,128)S(1)}, f32[1024,512]{1,0:T(8,128)}, u32[]{:S(2)}) copy-start(f32[1024,512]{1,0:T(8,128)} %gather_fusion.21) | copy-start | bytes 6291460
Sparse Core Ops, SparseCore 0:
  45.7 31.8 all-gather.2

commit v2 on v0

--- a/solution.py
+++ b/solution.py
@@ -117,9 +117,18 @@
     spread = jnp.sum(deviation * deviation, axis=-1) / time_total
     inverse = lax.rsqrt(spread + EPSILON)
     scaled = deviation * inverse[..., None]
-    scaled = lax.all_gather(scaled, "tm", axis=1, tiled=True)
     padded = jnp.pad(scaled, ((0, 0), (0, 0), (0, WMAX)))
-    window = lax.dynamic_slice_in_dim(padded, time_pos * block_len, block_len + WMAX, 2)
+    if time_parts == 2:
+        mine = lax.dynamic_slice_in_dim(padded, time_pos * block_len, block_len + WMAX, 2)
+        sent = lax.dynamic_slice_in_dim(padded, (1 - time_pos) * block_len, block_len + WMAX, 2)
+        theirs = lax.ppermute(sent, "tm", [(0, 1), (1, 0)])
+        first = time_pos == 0
+        window = jnp.concatenate(
+            [jnp.where(first, mine, theirs), jnp.where(first, theirs, mine)], axis=1
+        )
+    else:
+        padded = lax.all_gather(padded, "tm", axis=1, tiled=True)
+        window = lax.dynamic_slice_in_dim(padded, time_pos * block_len, block_len + WMAX, 2)
     running = jnp.cumsum(jnp.pad(window, ((0, 0), (0, 0), (1, 0))), axis=-1)
     leading_sum = running[..., :block_len]
     filtered = []

time: 128 us -> 127 us (level)
  blocking collectives: 2.18 us -> 0 us
  waiting for transfers between devices: 26 us -> 27.4 us
    all_gather x1 -> x0, blocking collectives: 2.18 us -> none  [body(): scaled = lax.all_gather(scaled, 'tm', axis=1, tiled=True)]
    ppermute x0 -> x1, waiting for transfers between devices: none -> 1.42 us  [body(): theirs = lax.ppermute(sent, 'tm', [(0, 1), (1, 0)])]
  transfers between devices with their start and end apart: 7 -> 8, of which waited for: 6 -> 7; matrix products, arithmetic and copies ran while one was open for 1% -> 1% of each run, Pallas kernels for 0% -> 0%
where the time goes in v2:
time: 127 us
  local copies, waits for them, and re-layouts  51.8 us (41%)
  waiting for transfers between devices  27.4 us (22%)
  other arithmetic  19.5 us (15%)
  between operations  16.5 us (13%)
  starting transfers between devices  11.8 us (9%)
    ppermute x6, waiting for transfers between devices, swapped(): return lax.ppermute(block, BANDS, route)  24.2 us
    slice x45, local copies, waits for them, and re-layouts, shift_rows(): result[..., step_size:]  11.8 us
    ppermute x6, starting transfers between devices, swapped(): return lax.ppermute(block, BANDS, route)  8.21 us
    gather x3, local copies, waits for them, and re-layouts, merge_across(): jnp.take(current, jnp.clip(lower_local, 0, rows_held - 1), axis=1)  7.46 us
    gather x9, local copies, waits for them, and re-layouts, merge_bands(): chosen = jnp.take(upper_flat, band_base + entries[1], axis=1)  7.02 us
    gather x9, local copies, waits for them, and re-layouts, merge_bands(): picked = jnp.take(lower_flat, band_base + entries[0], axis=1)  7.02 us
    select_n x36, other arithmetic, shift_rows(): result = jnp.where(flag[None, :, None], moved, result)  6.33 us
    gather x3, local copies, waits for them, and re-layouts, merge_across(): jnp.take(current, jnp.clip(upper_local, 0, rows_held - 1), axis=1)  6.32 us
  transfers between devices with their start and end apart: 8, of which 7 were waited for; matrix products, arithmetic and copies ran while one was open for 1% of the time, Pallas kernels for 0%

profile of v2, /device:TPU:0, one launch (start us, length us, event | category | flops | bytes accessed | tf_op | source)
XLA Modules:
  0.0 126.9 jit_solution(14413517985945664236)
XLA Ops:
  0.0 1.9 %copy.39 = bf16[1,1024,256]{2,0,1:T(2,128)(2,1)S(1)} copy(bf16[1,1024,256]{2,1,0:T(8,128)(2,1)} %param.15) | data formatting | bytes 1048576 | tf_op args[0]
  2.4 3.8 %reduce.63 = bf16[1024,256]{1,0:T(8,128)(2,1)S(1)} reduce(bf16[1024,1,256]{2,1,0:T(2,128)(2,1)S(1)} %bitcast.423, bf16[]{:T(256)} %broadcast.1530), dimensions={1}, to_apply=%bitcast.406.reduce_sub_computation | reduce | bytes 1048578
  6.2 0.9 reshape.1898
  7.1 3.5 %all-to-all-start = ((bf16[2,2,65536]{2,1,0:T(2,128)(2,1)}), bf16[2,2,65536]{2,1,0:T(2,128)(2,1)S(1)}, u32[]{:S(2)}, u32[]{:S(2)}) async-start(bf16[2,2,65536]{2,1,0:T(2,128)(2,1)} %reshape.1898), calls=%async_computation | async-start | bytes 1048576 | tf_op jit(solution)/shard_map/all_to_all | solution.py:102
  10.6 1.7 %all-to-all-done = bf16[2,2,65536]{2,1,0:T(2,128)(2,1)S(1)} async-done(((bf16[2,2,65536]{2,1,0:T(2,128)(2,1)}), bf16[2,2,65536]{2,1,0:T(2,128)(2,1)S(1)}, u32[]{:S(2)}, u32[]{:S(2)}) %all-to-all-start) | async-done | bytes 524320 | tf_op jit(solution)/shard_map/all_to_all | solution.py:102
  12.8 0.8 copy.38
  13.6 0.8 reshape.1502
  15.6 0.8 fusion.72
  16.5 1.0 gather_fusion
  17.4 1.0 gather_fusion.1
  19.3 0.8 gather_fusion.2
  20.0 0.8 gather_fusion.3
  21.6 0.8 gather_fusion.4
  22.3 0.8 gather_fusion.5
  23.5 0.8 gather_fusion.7
  24.6 0.8 gather_fusion.6
  25.7 0.8 gather_fusion.9
  27.0 0.8 gather_fusion.8
  27.9 0.8 gather_fusion.11
  29.4 0.8 gather_fusion.10
  30.3 0.8 gather_fusion.13
  32.0 0.8 gather_fusion.12
  32.9 0.8 gather_fusion.15
  34.9 0.8 gather_fusion.14
  35.8 0.8 gather_fusion.17
  38.0 0.8 gather_fusion.16
  38.9 1.0 gather_fusion.19
  42.2 1.0 gather_fusion.18
  43.8 1.2 collective-permute-done
  45.1 1.8 %gather_fusion.21 = f32[512,512]{1,0:T(8,128)S(1)} fusion(f32[128,512]{1,0:T(8,128)S(1)} %fusion.10, s32[1024]{0:T(1024)S(1)} %pad_clamp_fusion), kind=kCustom, calls=%fused_computation.22.clone | custom fusion | bytes 2099200 | tf_op jit(solution)/shard_map/jit(_take)/gather | solution.py:80
  50.7 0.9 slice.601
  51.7 1.6 %gather_fusion.20 = f32[512,512]{1,0:T(8,128)S(1)} fusion(f32[128,512]{1,0:T(8,128)S(1)} %fusion.10, s32[1024]{0:T(1024)S(1)} %pad_clamp_fusion.1), kind=kCustom, calls=%fused_computation.4.clone | custom fusion | bytes 2099200 | tf_op jit(solution)/shard_map/jit(_take)/gather | solution.py:77
  53.3 1.6 %fusion.3 = f32[1,512,512]{2,1,0:T(8,128)S(1)} fusion(f32[512,512]{1,0:T(8,128)S(1)} %gather_fusion.20, f32[1,512,512]{2,1,0:T(8,128)S(1)} %pad_select_fusion.8, f32[1,512,384]{2,1,0:T(8,128)} %slice.601, pred[512]{0:T(512)(128)(4,1)S(1)} %get-tuple-element.192, pred[512]{0:T(512)(128)(4,1)S(1)} %get-tuple-element.26, ...), kind=kLoop, calls=%fused_computation.40 | loop fusion | flops 1310720 | bytes 3934208 | tf_op jit(solution)/shard_map/add | solution.py:82
  55.2 1.8 %collective-permute-done.1 = f32[1,2,128,512]{3,2,1,0:T(8,128)S(1)} collective-permute-done((f32[1,2,128,512]{3,2,1,0:T(8,128)S(1)}, f32[1,2,128,512]{3,2,1,0:T(8,128)S(1)}, u32[]{:S(2)}, u32[]{:S(2)}) %collective-permute-start.1) | collective-permute-done | bytes 524320 | tf_op jit(solution)/shard_map/ppermute | solution.py:26
  57.0 3.1 %collective-permute-start.2 = (f32[1,1,128,512]{3,2,1,0:T(8,128)S(1)}, f32[1,1,128,512]{3,2,1,0:T(8,128)S(1)}, u32[]{:S(2)}, u32[]{:S(2)}) collective-permute-start(f32[1,1,128,512]{3,2,1,0:T(8,128)S(1)} %constant_dynamic-slice_fusion.22), channel_id=1, source_target_pairs={{0,8},{8,0},{4,12},{12,4},{16,24},{24,16},{20,28},{28,20},{1,9},{9... | collective-permute-start | bytes 786440 | tf_op jit(solution)/shard_map/ppermute | solution.py:26
  60.4 6.4 %collective-permute-done.2 = f32[1,1,128,512]{3,2,1,0:T(8,128)S(1)} collective-permute-done((f32[1,1,128,512]{3,2,1,0:T(8,128)S(1)}, f32[1,1,128,512]{3,2,1,0:T(8,128)S(1)}, u32[]{:S(2)}, u32[]{:S(2)}) %collective-permute-start.2) | collective-permute-done | bytes 262176 | tf_op jit(solution)/shard_map/ppermute | solution.py:26
  66.8 3.5 %gather_fusion.23 = f32[1024,512]{1,0:T(8,128)S(1)} fusion(f32[128,512]{1,0:T(8,128)S(1)} %add_bitcast_fusion, s32[1024]{0:T(1024)S(1)} %get-tuple-element.190), kind=kCustom, calls=%fused_computation.23.clone | custom fusion | bytes 4198400 | tf_op jit(solution)/shard_map/jit(_take)/gather | solution.py:80
  70.6 0.6 slice.602
  71.2 1.0 pad_select_fusion.7
  78.0 4.9 %gather_fusion.22 = f32[1024,512]{1,0:T(8,128)} fusion(f32[128,512]{1,0:T(8,128)S(1)} %add_bitcast_fusion, s32[1024]{0:T(1024)S(1)} %get-tuple-element.189), kind=kCustom, calls=%fused_computation.5.clone | custom fusion | bytes 4198400 | tf_op jit(solution)/shard_map/jit(_take)/gather | solution.py:77
  82.9 2.9 %fusion.1 = f32[1,1024,512]{2,1,0:T(8,128)S(1)} fusion(f32[1024,512]{1,0:T(8,128)} %gather_fusion.22, f32[1,1024,512]{2,1,0:T(8,128)S(1)} %pad_select_fusion, f32[1,1024,256]{2,1,0:T(8,128)S(1)} %slice.610, pred[1024]{0:T(1024)(128)(4,1)S(1)} %get-tuple-element.188, pred[1024]{0:T(1024)(128)(4,1)S(1)} %get-tuple-element.20, ...), kind=kLoop, calls=%fused_computation.27 | loop fusion | flops 2621440 | bytes 7344128 | tf_op jit(solution)/shard_map/add | solution.py:82
  86.0 2.6 %collective-permute-done.3 = f32[1,4,128,512]{3,2,1,0:T(8,128)S(1)} collective-permute-done((f32[1,4,128,512]{3,2,1,0:T(8,128)S(1)}, f32[1,4,128,512]{3,2,1,0:T(8,128)S(1)}, u32[]{:S(2)}, u32[]{:S(2)}) %collective-permute-start.3) | collective-permute-done | bytes 1048608 | tf_op jit(solution)/shard_map/ppermute | solution.py:26
  88.9 1.8 %collective-permute-start.4 = (f32[1,2,128,512]{3,2,1,0:T(8,128)S(1)}, f32[1,2,128,512]{3,2,1,0:T(8,128)S(1)}, u32[]{:S(2)}, u32[]{:S(2)}) collective-permute-start(f32[1,2,128,512]{3,2,1,0:T(8,128)S(1)} %dynamic-slice_bitcast_fusion.1), channel_id=1, source_target_pairs={{0,8},{8,0},{4,12},{12,4},{16,24},{24,16},{20,28},{28,20},{1,9},{9... | collective-permute-start | bytes 1572872 | tf_op jit(solution)/shard_map/ppermute | solution.py:26
  90.7 12.2 %collective-permute-done.4 = f32[1,2,128,512]{3,2,1,0:T(8,128)S(1)} collective-permute-done((f32[1,2,128,512]{3,2,1,0:T(8,128)S(1)}, f32[1,2,128,512]{3,2,1,0:T(8,128)S(1)}, u32[]{:S(2)}, u32[]{:S(2)}) %collective-permute-start.4) | collective-permute-done | bytes 524320 | tf_op jit(solution)/shard_map/ppermute | solution.py:26
  103.1 2.8 %collective-permute-start.5 = (f32[1,1,128,512]{3,2,1,0:T(8,128)S(1)}, f32[1,1,128,512]{3,2,1,0:T(8,128)S(1)}, u32[]{:S(2)}, u32[]{:S(2)}) collective-permute-start(f32[1,1,128,512]{3,2,1,0:T(8,128)S(1)} %constant_dynamic-slice_fusion.21), channel_id=1, source_target_pairs={{0,16},{16,0},{4,20},{20,4},{8,24},{24,8},{12,28},{28,12},{1,17},{... | collective-permute-start | bytes 786440 | tf_op jit(solution)/shard_map/ppermute | solution.py:26
  105.9 0.7 fusion.77
  122.0 1.4 %collective-permute-done.6 = f32[1,128,384]{2,1,0:T(8,128)S(1)} collective-permute-done((f32[1,128,384]{2,1,0:T(8,128)S(1)}, f32[1,128,384]{2,1,0:T(8,128)S(1)}, u32[]{:S(2)}, u32[]{:S(2)}) %collective-permute-start.6) | collective-permute-done | bytes 196640 | tf_op jit(solution)/shard_map/ppermute | solution.py:124
  125.0 2.0 %copy.31 = f32[1,256,8,256]{3,2,1,0:T(8,128)} copy(f32[1,256,8,256]{1,3,2,0:T(8,128)S(1)} %broadcast_multiply_fusion) | data formatting | bytes 4194304 | tf_op jit(solution)/shard_map/mul | solution.py:139
  (218 shorter events, 25.4 us)
Async XLA Ops:
  7.1 5.2 %all-to-all-start = ((bf16[2,2,65536]{2,1,0:T(2,128)(2,1)}), bf16[2,2,65536]{2,1,0:T(2,128)(2,1)S(1)}, u32[]{:S(2)}, u32[]{:S(2)}) async-start(bf16[2,2,65536]{2,1,0:T(2,128)(2,1)} %reshape.1898), calls=%async_computation | async-start | bytes 1048576 | tf_op jit(solution)/shard_map/all_to_all | solution.py:102
  13.6 2.0 %copy-start = (s32[3,12,2048]{2,1,0:T(8,128)S(1)}, s32[3,12,2048]{2,1,0:T(8,128)}, u32[]{:S(2)}) copy-start(s32[3,12,2048]{2,1,0:T(8,128)} %param.16) | copy-start | bytes 884740
  43.5 1.6 %collective-permute-start = (f32[1,1,128,512]{3,2,1,0:T(8,128)S(1)}, f32[1,1,128,512]{3,2,1,0:T(8,128)S(1)}, u32[]{:S(2)}, u32[]{:S(2)}) collective-permute-start(f32[1,1,128,512]{3,2,1,0:T(8,128)S(1)} %dynamic-slice_bitcast_fusion.3), channel_id=1, source_target_pairs={{0,4},{4,0},{8,12},{12,8},{16,20},{20,16},{24,28},{28,24},{1,5},{5... | collective-permute-start | bytes 786440 | tf_op jit(solution)/shard_map/ppermute | solution.py:26
  53.3 1.8 %copy-start.1 = (s32[3,1,2048]{2,1,0:T(1,128)S(1)}, s32[3,1,2048]{2,1,0:T(1,128)}, u32[]{:S(2)}) copy-start(s32[3,1,2048]{2,1,0:T(1,128)} %get-tuple-element.85) | copy-start | bytes 73732
  54.9 2.0 %collective-permute-start.1 = (f32[1,2,128,512]{3,2,1,0:T(8,128)S(1)}, f32[1,2,128,512]{3,2,1,0:T(8,128)S(1)}, u32[]{:S(2)}, u32[]{:S(2)}) collective-permute-start(f32[1,2,128,512]{3,2,1,0:T(8,128)S(1)} %dynamic-slice_bitcast_fusion.2), channel_id=1, source_target_pairs={{0,4},{4,0},{8,12},{12,8},{16,20},{20,16},{24,28},{28,24},{1,5},{5... | collective-permute-start | bytes 1572872 | tf_op jit(solution)/shard_map/ppermute | solution.py:26
  57.0 9.7 %collective-permute-start.2 = (f32[1,1,128,512]{3,2,1,0:T(8,128)S(1)}, f32[1,1,128,512]{3,2,1,0:T(8,128)S(1)}, u32[]{:S(2)}, u32[]{:S(2)}) collective-permute-start(f32[1,1,128,512]{3,2,1,0:T(8,128)S(1)} %constant_dynamic-slice_fusion.22), channel_id=1, source_target_pairs={{0,8},{8,0},{4,12},{12,4},{16,24},{24,16},{20,28},{28,20},{1,9},{9... | collective-permute-start | bytes 786440 | tf_op jit(solution)/shard_map/ppermute | solution.py:26
  85.9 2.7 %collective-permute-start.3 = (f32[1,4,128,512]{3,2,1,0:T(8,128)S(1)}, f32[1,4,128,512]{3,2,1,0:T(8,128)S(1)}, u32[]{:S(2)}, u32[]{:S(2)}) collective-permute-start(f32[1,4,128,512]{3,2,1,0:T(8,128)S(1)} %dynamic-slice_bitcast_fusion), channel_id=1, source_target_pairs={{0,4},{4,0},{8,12},{12,8},{16,20},{20,16},{24,28},{28,24},{1,5},{5... | collective-permute-start | bytes 3145736 | tf_op jit(solution)/shard_map/ppermute | solution.py:26
  88.8 17.0 %copy-start.2 = (s32[8]{0:T(128)S(1)}, s32[8]{0:T(128)}, u32[]{:S(2)}) copy-start(s32[8]{0:T(128)} %param.17) | copy-start | bytes 100
  88.9 14.0 %collective-permute-start.4 = (f32[1,2,128,512]{3,2,1,0:T(8,128)S(1)}, f32[1,2,128,512]{3,2,1,0:T(8,128)S(1)}, u32[]{:S(2)}, u32[]{:S(2)}) collective-permute-start(f32[1,2,128,512]{3,2,1,0:T(8,128)S(1)} %dynamic-slice_bitcast_fusion.1), channel_id=1, source_target_pairs={{0,8},{8,0},{4,12},{12,4},{16,24},{24,16},{20,28},{28,20},{1,9},{9... | collective-permute-start | bytes 1572872 | tf_op jit(solution)/shard_map/ppermute | solution.py:26
  103.1 18.3 %collective-permute-start.5 = (f32[1,1,128,512]{3,2,1,0:T(8,128)S(1)}, f32[1,1,128,512]{3,2,1,0:T(8,128)S(1)}, u32[]{:S(2)}, u32[]{:S(2)}) collective-permute-start(f32[1,1,128,512]{3,2,1,0:T(8,128)S(1)} %constant_dynamic-slice_fusion.21), channel_id=1, source_target_pairs={{0,16},{16,0},{4,20},{20,4},{8,24},{24,8},{12,28},{28,12},{1,17},{... | collective-permute-start | bytes 786440 | tf_op jit(solution)/shard_map/ppermute | solution.py:26
  121.9 1.5 %collective-permute-start.6 = (f32[1,128,384]{2,1,0:T(8,128)S(1)}, f32[1,128,384]{2,1,0:T(8,128)S(1)}, u32[]{:S(2)}, u32[]{:S(2)}) collective-permute-start(f32[1,128,384]{2,1,0:T(8,128)S(1)} %pad_dynamic-slice_fusion), channel_id=1, source_target_pairs={{0,4},{4,0},{1,5},{5,1},{2,6},{6,2},{3,7},{7,3},{8,12},{12,8},{9,1... | collective-permute-start | bytes 589832 | tf_op jit(solution)/shard_map/ppermute | solution.py:124

commit v3 on v2

--- a/solution.py
+++ b/solution.py
@@ -99,10 +99,10 @@
     time_pos = lax.axis_index("tm")
     device_pos = lax.axis_index("freq") * time_parts + time_pos
     block_len = intensity.shape[2]
-    whole_rows = lax.all_to_all(intensity, "tm", 1, 2, tiled=True)
+    whole_rows = lax.all_to_all(intensity.astype(jnp.float32), "tm", 1, 2, tiled=True)
     beam_count, channels_held, time_total = whole_rows.shape
     local_levels = channels_held.bit_length() - 1
-    current = whole_rows.astype(jnp.float32)[:, :, None, :]
+    current = whole_rows[:, :, None, :]
     for merge_level in range(1, local_levels + 1):
         current = merge_bands(
             current, delay_tables, merge_level, device_pos * (channels_held >> merge_level)

time: 127 us -> 123 us (0.969)
  other arithmetic: 19.5 us -> 15.7 us
    unnamed x8 -> x7, other arithmetic: 4.18 us -> 0.33 us
    unnamed x11 -> x7, local copies, waits for them, and re-layouts: 3.9 us -> 0.18 us
    convert_element_type x2 -> x1, local copies, waits for them, and re-layouts: 1.65 us -> 2.82 us  [body(): intensity.astype(jnp.float32)]
where the time goes in v3:
time: 123 us
  local copies, waits for them, and re-layouts  50.9 us (41%)
  waiting for transfers between devices  27.7 us (23%)
  between operations  16.5 us (13%)
  other arithmetic  15.7 us (13%)
  starting transfers between devices  11.9 us (10%)
    ppermute x6, waiting for transfers between devices, swapped(): return lax.ppermute(block, BANDS, route)  24.2 us
    slice x45, local copies, waits for them, and re-layouts, shift_rows(): result[..., step_size:]  11.8 us
    ppermute x6, starting transfers between devices, swapped(): return lax.ppermute(block, BANDS, route)  8.21 us
    gather x3, local copies, waits for them, and re-layouts, merge_across(): jnp.take(current, jnp.clip(lower_local, 0, rows_held - 1), axis=1)  7.46 us
    gather x9, local copies, waits for them, and re-layouts, merge_bands(): picked = jnp.take(lower_flat, band_base + entries[0], axis=1)  7.02 us
    gather x9, local copies, waits for them, and re-layouts, merge_bands(): chosen = jnp.take(upper_flat, band_base + entries[1], axis=1)  7.02 us
    select_n x36, other arithmetic, shift_rows(): result = jnp.where(flag[None, :, None], moved, result)  6.33 us
    gather x3, local copies, waits for them, and re-layouts, merge_across(): jnp.take(current, jnp.clip(upper_local, 0, rows_held - 1), axis=1)  6.32 us
  transfers between devices with their start and end apart: 8, of which 7 were waited for; matrix products, arithmetic and copies ran while one was open for 1% of the time, Pallas kernels for 0%

profile of v3, /device:TPU:0, one launch (start us, length us, event | category | flops | bytes accessed | tf_op | source)
XLA Modules:
  0.0 122.6 jit_solution(12467130014793362067)
XLA Ops:
  0.0 2.8 %copy.32 = f32[1,1024,256]{2,0,1:T(1,128)} copy(bf16[1,1024,256]{2,1,0:T(8,128)(2,1)} %param.15) | data formatting | bytes 1572864 | tf_op jit(solution)/shard_map/convert_element_type | solution.py:102
  2.8 3.6 %all-to-all-start = ((f32[1,1024,256]{2,0,1:T(1,128)}), f32[1,1024,256]{2,0,1:T(1,128)S(1)}, u32[]{:S(2)}, u32[]{:S(2)}) async-start(f32[1,1024,256]{2,0,1:T(1,128)} %copy.32), calls=%async_computation | async-start | bytes 2097152 | tf_op jit(solution)/shard_map/all_to_all | solution.py:102
  6.4 2.1 %all-to-all-done = f32[1,1024,256]{2,0,1:T(1,128)S(1)} async-done(((f32[1,1024,256]{2,0,1:T(1,128)}), f32[1,1024,256]{2,0,1:T(1,128)S(1)}, u32[]{:S(2)}, u32[]{:S(2)}) %all-to-all-start) | async-done | bytes 1048608 | tf_op jit(solution)/shard_map/all_to_all | solution.py:102
  8.5 0.8 copy.43
  9.3 0.8 broadcast_in_dim.430
  11.3 0.8 fusion.72
  12.2 1.0 gather_fusion
  13.2 1.0 gather_fusion.1
  15.0 0.8 gather_fusion.2
  15.7 0.8 gather_fusion.3
  17.3 0.8 gather_fusion.4
  18.0 0.8 gather_fusion.5
  19.2 0.8 gather_fusion.7
  20.3 0.8 gather_fusion.6
  21.4 0.8 gather_fusion.9
  22.7 0.8 gather_fusion.8
  23.6 0.8 gather_fusion.11
  25.1 0.8 gather_fusion.10
  26.0 0.8 gather_fusion.13
  27.7 0.8 gather_fusion.12
  28.6 0.8 gather_fusion.15
  30.6 0.8 gather_fusion.14
  31.5 0.8 gather_fusion.17
  33.8 0.8 gather_fusion.16
  34.6 1.0 gather_fusion.19
  37.9 1.0 gather_fusion.18
  39.6 1.2 %collective-permute-done = f32[1,1,128,512]{3,2,1,0:T(8,128)S(1)} collective-permute-done((f32[1,1,128,512]{3,2,1,0:T(8,128)S(1)}, f32[1,1,128,512]{3,2,1,0:T(8,128)S(1)}, u32[]{:S(2)}, u32[]{:S(2)}) %collective-permute-start) | collective-permute-done | bytes 262176 | tf_op jit(solution)/shard_map/ppermute | solution.py:26
  40.8 1.8 %gather_fusion.21 = f32[512,512]{1,0:T(8,128)S(1)} fusion(f32[128,512]{1,0:T(8,128)S(1)} %fusion.10, s32[1024]{0:T(1024)S(1)} %pad_clamp_fusion), kind=kCustom, calls=%fused_computation.22.clone | custom fusion | bytes 2099200 | tf_op jit(solution)/shard_map/jit(_take)/gather | solution.py:80
  46.5 0.9 slice.601
  47.4 1.6 %gather_fusion.20 = f32[512,512]{1,0:T(8,128)S(1)} fusion(f32[128,512]{1,0:T(8,128)S(1)} %fusion.10, s32[1024]{0:T(1024)S(1)} %pad_clamp_fusion.1), kind=kCustom, calls=%fused_computation.4.clone | custom fusion | bytes 2099200 | tf_op jit(solution)/shard_map/jit(_take)/gather | solution.py:77
  49.0 1.6 %fusion.3 = f32[1,512,512]{2,1,0:T(8,128)S(1)} fusion(f32[512,512]{1,0:T(8,128)S(1)} %gather_fusion.20, f32[1,512,512]{2,1,0:T(8,128)S(1)} %pad_select_fusion.8, f32[1,512,384]{2,1,0:T(8,128)} %slice.601, pred[512]{0:T(512)(128)(4,1)S(1)} %get-tuple-element.192, pred[512]{0:T(512)(128)(4,1)S(1)} %get-tuple-element.26, ...), kind=kLoop, calls=%fused_computation.40 | loop fusion | flops 1310720 | bytes 3934208 | tf_op jit(solution)/shard_map/add | solution.py:82
  50.9 1.8 %collective-permute-done.1 = f32[1,2,128,512]{3,2,1,0:T(8,128)S(1)} collective-permute-done((f32[1,2,128,512]{3,2,1,0:T(8,128)S(1)}, f32[1,2,128,512]{3,2,1,0:T(8,128)S(1)}, u32[]{:S(2)}, u32[]{:S(2)}) %collective-permute-start.1) | collective-permute-done | bytes 524320 | tf_op jit(solution)/shard_map/ppermute | solution.py:26
  52.8 3.1 %collective-permute-start.2 = (f32[1,1,128,512]{3,2,1,0:T(8,128)S(1)}, f32[1,1,128,512]{3,2,1,0:T(8,128)S(1)}, u32[]{:S(2)}, u32[]{:S(2)}) collective-permute-start(f32[1,1,128,512]{3,2,1,0:T(8,128)S(1)} %constant_dynamic-slice_fusion.22), channel_id=1, source_target_pairs={{0,8},{8,0},{4,12},{12,4},{16,24},{24,16},{20,28},{28,20},{1,9},{9... | collective-permute-start | bytes 786440 | tf_op jit(solution)/shard_map/ppermute | solution.py:26
  56.1 6.4 %collective-permute-done.2 = f32[1,1,128,512]{3,2,1,0:T(8,128)S(1)} collective-permute-done((f32[1,1,128,512]{3,2,1,0:T(8,128)S(1)}, f32[1,1,128,512]{3,2,1,0:T(8,128)S(1)}, u32[]{:S(2)}, u32[]{:S(2)}) %collective-permute-start.2) | collective-permute-done | bytes 262176 | tf_op jit(solution)/shard_map/ppermute | solution.py:26
  62.5 3.5 %gather_fusion.23 = f32[1024,512]{1,0:T(8,128)S(1)} fusion(f32[128,512]{1,0:T(8,128)S(1)} %add_bitcast_fusion, s32[1024]{0:T(1024)S(1)} %get-tuple-element.190), kind=kCustom, calls=%fused_computation.23.clone | custom fusion | bytes 4198400 | tf_op jit(solution)/shard_map/jit(_take)/gather | solution.py:80
  66.9 1.0 pad_select_fusion.7
  68.8 0.6 slice.604
  69.7 0.6 slice.605
  70.6 0.6 slice.606
  73.8 4.9 %gather_fusion.22 = f32[1024,512]{1,0:T(8,128)} fusion(f32[128,512]{1,0:T(8,128)S(1)} %add_bitcast_fusion, s32[1024]{0:T(1024)S(1)} %get-tuple-element.189), kind=kCustom, calls=%fused_computation.5.clone | custom fusion | bytes 4198400 | tf_op jit(solution)/shard_map/jit(_take)/gather | solution.py:77
  78.6 2.9 %fusion.1 = f32[1,1024,512]{2,1,0:T(8,128)S(1)} fusion(f32[1024,512]{1,0:T(8,128)} %gather_fusion.22, f32[1,1024,512]{2,1,0:T(8,128)S(1)} %pad_select_fusion, f32[1,1024,256]{2,1,0:T(8,128)S(1)} %slice.610, pred[1024]{0:T(1024)(128)(4,1)S(1)} %get-tuple-element.188, pred[1024]{0:T(1024)(128)(4,1)S(1)} %get-tuple-element.20, ...), kind=kLoop, calls=%fused_computation.27 | loop fusion | flops 2621440 | bytes 7344128 | tf_op jit(solution)/shard_map/add | solution.py:82
  81.7 2.6 %collective-permute-done.3 = f32[1,4,128,512]{3,2,1,0:T(8,128)S(1)} collective-permute-done((f32[1,4,128,512]{3,2,1,0:T(8,128)S(1)}, f32[1,4,128,512]{3,2,1,0:T(8,128)S(1)}, u32[]{:S(2)}, u32[]{:S(2)}) %collective-permute-start.3) | collective-permute-done | bytes 1048608 | tf_op jit(solution)/shard_map/ppermute | solution.py:26
  84.6 1.8 %collective-permute-start.4 = (f32[1,2,128,512]{3,2,1,0:T(8,128)S(1)}, f32[1,2,128,512]{3,2,1,0:T(8,128)S(1)}, u32[]{:S(2)}, u32[]{:S(2)}) collective-permute-start(f32[1,2,128,512]{3,2,1,0:T(8,128)S(1)} %dynamic-slice_bitcast_fusion.1), channel_id=1, source_target_pairs={{0,8},{8,0},{4,12},{12,4},{16,24},{24,16},{20,28},{28,20},{1,9},{9... | collective-permute-start | bytes 1572872 | tf_op jit(solution)/shard_map/ppermute | solution.py:26
  86.4 12.2 %collective-permute-done.4 = f32[1,2,128,512]{3,2,1,0:T(8,128)S(1)} collective-permute-done((f32[1,2,128,512]{3,2,1,0:T(8,128)S(1)}, f32[1,2,128,512]{3,2,1,0:T(8,128)S(1)}, u32[]{:S(2)}, u32[]{:S(2)}) %collective-permute-start.4) | collective-permute-done | bytes 524320 | tf_op jit(solution)/shard_map/ppermute | solution.py:26
  98.8 2.8 %collective-permute-start.5 = (f32[1,1,128,512]{3,2,1,0:T(8,128)S(1)}, f32[1,1,128,512]{3,2,1,0:T(8,128)S(1)}, u32[]{:S(2)}, u32[]{:S(2)}) collective-permute-start(f32[1,1,128,512]{3,2,1,0:T(8,128)S(1)} %constant_dynamic-slice_fusion.21), channel_id=1, source_target_pairs={{0,16},{16,0},{4,20},{20,4},{8,24},{24,8},{12,28},{28,12},{1,17},{... | collective-permute-start | bytes 786440 | tf_op jit(solution)/shard_map/ppermute | solution.py:26
  101.6 0.7 fusion.77
  117.7 1.4 %collective-permute-done.6 = f32[1,128,384]{2,1,0:T(8,128)S(1)} collective-permute-done((f32[1,128,384]{2,1,0:T(8,128)S(1)}, f32[1,128,384]{2,1,0:T(8,128)S(1)}, u32[]{:S(2)}, u32[]{:S(2)}) %collective-permute-start.6) | collective-permute-done | bytes 196640 | tf_op jit(solution)/shard_map/ppermute | solution.py:124
  120.7 2.0 %copy.37 = f32[1,256,8,256]{3,2,1,0:T(8,128)} copy(f32[1,256,8,256]{1,3,2,0:T(8,128)S(1)} %broadcast_multiply_fusion) | data formatting | bytes 4194304 | tf_op jit(solution)/shard_map/mul | solution.py:139
  (214 shorter events, 23.1 us)
Async XLA Ops:
  2.8 5.7 %all-to-all-start = ((f32[1,1024,256]{2,0,1:T(1,128)}), f32[1,1024,256]{2,0,1:T(1,128)S(1)}, u32[]{:S(2)}, u32[]{:S(2)}) async-start(f32[1,1024,256]{2,0,1:T(1,128)} %copy.32), calls=%async_computation | async-start | bytes 2097152 | tf_op jit(solution)/shard_map/all_to_all | solution.py:102
  9.3 2.0 %copy-start = (s32[3,12,2048]{2,1,0:T(8,128)S(1)}, s32[3,12,2048]{2,1,0:T(8,128)}, u32[]{:S(2)}) copy-start(s32[3,12,2048]{2,1,0:T(8,128)} %param.16) | copy-start | bytes 884740
  39.2 1.6 %collective-permute-start = (f32[1,1,128,512]{3,2,1,0:T(8,128)S(1)}, f32[1,1,128,512]{3,2,1,0:T(8,128)S(1)}, u32[]{:S(2)}, u32[]{:S(2)}) collective-permute-start(f32[1,1,128,512]{3,2,1,0:T(8,128)S(1)} %dynamic-slice_bitcast_fusion.3), channel_id=1, source_target_pairs={{0,4},{4,0},{8,12},{12,8},{16,20},{20,16},{24,28},{28,24},{1,5},{5... | collective-permute-start | bytes 786440 | tf_op jit(solution)/shard_map/ppermute | solution.py:26
  49.0 1.8 %copy-start.1 = (s32[3,1,2048]{2,1,0:T(1,128)S(1)}, s32[3,1,2048]{2,1,0:T(1,128)}, u32[]{:S(2)}) copy-start(s32[3,1,2048]{2,1,0:T(1,128)} %get-tuple-element.85) | copy-start | bytes 73732
  50.7 2.0 %collective-permute-start.1 = (f32[1,2,128,512]{3,2,1,0:T(8,128)S(1)}, f32[1,2,128,512]{3,2,1,0:T(8,128)S(1)}, u32[]{:S(2)}, u32[]{:S(2)}) collective-permute-start(f32[1,2,128,512]{3,2,1,0:T(8,128)S(1)} %dynamic-slice_bitcast_fusion.2), channel_id=1, source_target_pairs={{0,4},{4,0},{8,12},{12,8},{16,20},{20,16},{24,28},{28,24},{1,5},{5... | collective-permute-start | bytes 1572872 | tf_op jit(solution)/shard_map/ppermute | solution.py:26
  52.8 9.7 %collective-permute-start.2 = (f32[1,1,128,512]{3,2,1,0:T(8,128)S(1)}, f32[1,1,128,512]{3,2,1,0:T(8,128)S(1)}, u32[]{:S(2)}, u32[]{:S(2)}) collective-permute-start(f32[1,1,128,512]{3,2,1,0:T(8,128)S(1)} %constant_dynamic-slice_fusion.22), channel_id=1, source_target_pairs={{0,8},{8,0},{4,12},{12,4},{16,24},{24,16},{20,28},{28,20},{1,9},{9... | collective-permute-start | bytes 786440 | tf_op jit(solution)/shard_map/ppermute | solution.py:26
  81.6 2.7 %collective-permute-start.3 = (f32[1,4,128,512]{3,2,1,0:T(8,128)S(1)}, f32[1,4,128,512]{3,2,1,0:T(8,128)S(1)}, u32[]{:S(2)}, u32[]{:S(2)}) collective-permute-start(f32[1,4,128,512]{3,2,1,0:T(8,128)S(1)} %dynamic-slice_bitcast_fusion), channel_id=1, source_target_pairs={{0,4},{4,0},{8,12},{12,8},{16,20},{20,16},{24,28},{28,24},{1,5},{5... | collective-permute-start | bytes 3145736 | tf_op jit(solution)/shard_map/ppermute | solution.py:26
  84.6 17.0 %copy-start.2 = (s32[8]{0:T(128)S(1)}, s32[8]{0:T(128)}, u32[]{:S(2)}) copy-start(s32[8]{0:T(128)} %param.17) | copy-start | bytes 100
  84.6 14.0 %collective-permute-start.4 = (f32[1,2,128,512]{3,2,1,0:T(8,128)S(1)}, f32[1,2,128,512]{3,2,1,0:T(8,128)S(1)}, u32[]{:S(2)}, u32[]{:S(2)}) collective-permute-start(f32[1,2,128,512]{3,2,1,0:T(8,128)S(1)} %dynamic-slice_bitcast_fusion.1), channel_id=1, source_target_pairs={{0,8},{8,0},{4,12},{12,4},{16,24},{24,16},{20,28},{28,20},{1,9},{9... | collective-permute-start | bytes 1572872 | tf_op jit(solution)/shard_map/ppermute | solution.py:26
  98.8 18.3 %collective-permute-start.5 = (f32[1,1,128,512]{3,2,1,0:T(8,128)S(1)}, f32[1,1,128,512]{3,2,1,0:T(8,128)S(1)}, u32[]{:S(2)}, u32[]{:S(2)}) collective-permute-start(f32[1,1,128,512]{3,2,1,0:T(8,128)S(1)} %constant_dynamic-slice_fusion.21), channel_id=1, source_target_pairs={{0,16},{16,0},{4,20},{20,4},{8,24},{24,8},{12,28},{28,12},{1,17},{... | collective-permute-start | bytes 786440 | tf_op jit(solution)/shard_map/ppermute | solution.py:26
  117.6 1.5 %collective-permute-start.6 = (f32[1,128,384]{2,1,0:T(8,128)S(1)}, f32[1,128,384]{2,1,0:T(8,128)S(1)}, u32[]{:S(2)}, u32[]{:S(2)}) collective-permute-start(f32[1,128,384]{2,1,0:T(8,128)S(1)} %pad_dynamic-slice_fusion), channel_id=1, source_target_pairs={{0,4},{4,0},{1,5},{5,1},{2,6},{6,2},{3,7},{7,3},{8,12},{12,8},{9,1... | collective-permute-start | bytes 589832 | tf_op jit(solution)/shard_map/ppermute | solution.py:124

commit v4 on v3

--- a/solution.py
+++ b/solution.py
@@ -82,14 +82,17 @@
     partial_value = jnp.where(lower_hit[None, :, None], lower_rows, 0.0) + jnp.where(
         upper_hit[None, :, None], upper_rows, 0.0
     )
-    for bit_index in range(cross_step + 1):
-        blocks = partial_value.shape[1] // rows_held
-        paired = partial_value.reshape(beam_count, blocks // 2, 2, rows_held, columns)
+    remaining = list(range(cross_step + 1))
+    for bit_index in [0] + list(range(cross_step, 0, -1)):
+        place = remaining.index(bit_index)
+        remaining.remove(bit_index)
+        below = 2**place * rows_held
+        paired = partial_value.reshape(beam_count, -1, 2, below, columns)
         chosen_bit = device_pos >> bit_index & 1
         kept_rows = lax.dynamic_index_in_dim(paired, chosen_bit, 2, keepdims=False)
         given_rows = lax.dynamic_index_in_dim(paired, 1 - chosen_bit, 2, keepdims=False)
         partial_value = (kept_rows + swapped(given_rows, bit_index)).reshape(
-            beam_count, blocks // 2 * rows_held, columns
+            beam_count, -1, columns
         )
     return partial_value
 

time: 123 us -> 136 us (1.11)
  waiting for transfers between devices: 27.7 us -> 39 us
    ppermute x6, waiting for transfers between devices: 24.2 us -> 35.5 us  [swapped(): return lax.ppermute(block, BANDS, route)]
where the time goes in v4:
time: 136 us; the launch traced here: 135 us
  local copies, waits for them, and re-layouts  52.2 us (38%)
  waiting for transfers between devices  39 us (29%)
  other arithmetic  16.9 us (12%)
  between operations  16.5 us (12%)
  starting transfers between devices  10.8 us (8%)
    ppermute x6, waiting for transfers between devices, swapped(): return lax.ppermute(block, BANDS, route)  35.5 us
    slice x45, local copies, waits for them, and re-layouts, shift_rows(): result[..., step_size:]  11.8 us
    gather x3, local copies, waits for them, and re-layouts, merge_across(): jnp.take(current, jnp.clip(lower_local, 0, rows_held - 1), axis=1)  7.46 us
    ppermute x6, starting transfers between devices, swapped(): return lax.ppermute(block, BANDS, route)  7.2 us
    gather x9, local copies, waits for them, and re-layouts, merge_bands(): picked = jnp.take(lower_flat, band_base + entries[0], axis=1)  7.02 us
    gather x9, local copies, waits for them, and re-layouts, merge_bands(): chosen = jnp.take(upper_flat, band_base + entries[1], axis=1)  7.02 us
    select_n x36, other arithmetic, shift_rows(): result = jnp.where(flag[None, :, None], moved, result)  6.33 us
    gather x3, local copies, waits for them, and re-layouts, merge_across(): jnp.take(current, jnp.clip(upper_local, 0, rows_held - 1), axis=1)  6.32 us
  transfers between devices with their start and end apart: 8, of which 7 were waited for; matrix products, arithmetic and copies ran while one was open for 1% of the time, Pallas kernels for 0%

profile of v4, /device:TPU:0, one launch (start us, length us, event | category | flops | bytes accessed | tf_op | source)
XLA Modules:
  0.0 135.4 jit_solution(12900443366239893116)
XLA Ops:
  0.0 2.8 %copy.32 = f32[1,1024,256]{2,0,1:T(1,128)} copy(bf16[1,1024,256]{2,1,0:T(8,128)(2,1)} %param.15) | data formatting | bytes 1572864 | tf_op jit(solution)/shard_map/convert_element_type | solution.py:105
  2.8 3.6 %all-to-all-start = ((f32[1,1024,256]{2,0,1:T(1,128)}), f32[1,1024,256]{2,0,1:T(1,128)S(1)}, u32[]{:S(2)}, u32[]{:S(2)}) async-start(f32[1,1024,256]{2,0,1:T(1,128)} %copy.32), calls=%async_computation | async-start | bytes 2097152 | tf_op jit(solution)/shard_map/all_to_all | solution.py:105
  6.4 2.1 %all-to-all-done = f32[1,1024,256]{2,0,1:T(1,128)S(1)} async-done(((f32[1,1024,256]{2,0,1:T(1,128)}), f32[1,1024,256]{2,0,1:T(1,128)S(1)}, u32[]{:S(2)}, u32[]{:S(2)}) %all-to-all-start) | async-done | bytes 1048608 | tf_op jit(solution)/shard_map/all_to_all | solution.py:105
  8.5 0.8 copy.43
  9.3 0.8 broadcast_in_dim.430
  11.3 0.8 fusion.72
  12.2 1.0 gather_fusion
  13.2 1.0 gather_fusion.1
  15.0 0.8 gather_fusion.2
  15.7 0.8 gather_fusion.3
  17.3 0.8 gather_fusion.4
  18.0 0.8 gather_fusion.5
  19.2 0.8 gather_fusion.7
  20.3 0.8 gather_fusion.6
  21.4 0.8 gather_fusion.9
  22.7 0.8 gather_fusion.8
  23.6 0.8 gather_fusion.11
  25.1 0.8 gather_fusion.10
  26.0 0.8 gather_fusion.13
  27.7 0.8 gather_fusion.12
  28.6 0.8 gather_fusion.15
  30.6 0.8 gather_fusion.14
  31.5 0.8 gather_fusion.17
  33.8 0.8 gather_fusion.16
  34.6 1.0 gather_fusion.19
  37.9 1.0 gather_fusion.18
  39.6 1.2 collective-permute-done
  40.8 1.8 %gather_fusion.21 = f32[512,512]{1,0:T(8,128)S(1)} fusion(f32[128,512]{1,0:T(8,128)S(1)} %fusion.10, s32[1024]{0:T(1024)S(1)} %pad_clamp_fusion), kind=kCustom, calls=%fused_computation.22.clone | custom fusion | bytes 2099200 | tf_op jit(solution)/shard_map/jit(_take)/gather | solution.py:80
  46.5 0.9 slice.601
  47.4 1.6 %gather_fusion.20 = f32[512,512]{1,0:T(8,128)S(1)} fusion(f32[128,512]{1,0:T(8,128)S(1)} %fusion.10, s32[1024]{0:T(1024)S(1)} %pad_clamp_fusion.1), kind=kCustom, calls=%fused_computation.4.clone | custom fusion | bytes 2099200 | tf_op jit(solution)/shard_map/jit(_take)/gather | solution.py:77
  49.0 1.6 %fusion.3 = f32[1,512,512]{2,1,0:T(8,128)S(1)} fusion(f32[512,512]{1,0:T(8,128)S(1)} %gather_fusion.20, f32[1,512,512]{2,1,0:T(8,128)S(1)} %pad_select_fusion.8, f32[1,512,384]{2,1,0:T(8,128)} %slice.601, pred[512]{0:T(512)(128)(4,1)S(1)} %get-tuple-element.192, pred[512]{0:T(512)(128)(4,1)S(1)} %get-tuple-element.26, ...), kind=kLoop, calls=%fused_computation.40 | loop fusion | flops 1310720 | bytes 3934208 | tf_op jit(solution)/shard_map/add | solution.py:82
  50.9 1.8 %collective-permute-done.1 = f32[1,2,128,512]{3,2,1,0:T(8,128)S(1)} collective-permute-done((f32[1,2,128,512]{3,2,1,0:T(8,128)S(1)}, f32[1,2,128,512]{3,2,1,0:T(8,128)S(1)}, u32[]{:S(2)}, u32[]{:S(2)}) %collective-permute-start.1) | collective-permute-done | bytes 524320 | tf_op jit(solution)/shard_map/ppermute | solution.py:26
  52.8 3.1 %collective-permute-start.2 = (f32[1,1,128,512]{3,2,1,0:T(8,128)S(1)}, f32[1,1,128,512]{3,2,1,0:T(8,128)S(1)}, u32[]{:S(2)}, u32[]{:S(2)}) collective-permute-start(f32[1,1,128,512]{3,2,1,0:T(8,128)S(1)} %constant_dynamic-slice_fusion.21), channel_id=1, source_target_pairs={{0,8},{8,0},{4,12},{12,4},{16,24},{24,16},{20,28},{28,20},{1,9},{9... | collective-permute-start | bytes 786440 | tf_op jit(solution)/shard_map/ppermute | solution.py:26
  56.1 6.4 %collective-permute-done.2 = f32[1,1,128,512]{3,2,1,0:T(8,128)S(1)} collective-permute-done((f32[1,1,128,512]{3,2,1,0:T(8,128)S(1)}, f32[1,1,128,512]{3,2,1,0:T(8,128)S(1)}, u32[]{:S(2)}, u32[]{:S(2)}) %collective-permute-start.2) | collective-permute-done | bytes 262176 | tf_op jit(solution)/shard_map/ppermute | solution.py:26
  62.5 3.5 %gather_fusion.23 = f32[1024,512]{1,0:T(8,128)S(1)} fusion(f32[128,512]{1,0:T(8,128)S(1)} %add_bitcast_fusion, s32[1024]{0:T(1024)S(1)} %get-tuple-element.190), kind=kCustom, calls=%fused_computation.23.clone | custom fusion | bytes 4198400 | tf_op jit(solution)/shard_map/jit(_take)/gather | solution.py:80
  66.3 0.6 slice.602
  66.9 1.0 pad_select_fusion.7
  73.8 4.9 %gather_fusion.22 = f32[1024,512]{1,0:T(8,128)} fusion(f32[128,512]{1,0:T(8,128)S(1)} %add_bitcast_fusion, s32[1024]{0:T(1024)S(1)} %get-tuple-element.189), kind=kCustom, calls=%fused_computation.5.clone | custom fusion | bytes 4198400 | tf_op jit(solution)/shard_map/jit(_take)/gather | solution.py:77
  78.6 2.9 %fusion.1 = f32[1,1024,512]{2,1,0:T(8,128)S(1)} fusion(f32[1024,512]{1,0:T(8,128)} %gather_fusion.22, f32[1,1024,512]{2,1,0:T(8,128)S(1)} %pad_select_fusion, f32[1,1024,256]{2,1,0:T(8,128)S(1)} %slice.610, pred[1024]{0:T(1024)(128)(4,1)S(1)} %get-tuple-element.188, pred[1024]{0:T(1024)(128)(4,1)S(1)} %get-tuple-element.20, ...), kind=kLoop, calls=%fused_computation.27 | loop fusion | flops 2621440 | bytes 7344128 | tf_op jit(solution)/shard_map/add | solution.py:82
  81.5 1.3 copy-done
  83.0 2.6 %collective-permute-done.3 = f32[1,4,128,512]{3,2,1,0:T(8,128)S(1)} collective-permute-done((f32[1,4,128,512]{3,2,1,0:T(8,128)S(1)}, f32[1,4,128,512]{3,2,1,0:T(8,128)S(1)}, u32[]{:S(2)}, u32[]{:S(2)}) %collective-permute-start.3) | collective-permute-done | bytes 1048608 | tf_op jit(solution)/shard_map/ppermute | solution.py:26
  85.7 1.4 %bitcast_add_fusion = f32[1,4,128,512]{3,2,1,0:T(8,128)S(1)} fusion(f32[1,4,128,512]{3,2,1,0:T(8,128)S(1)} %collective-permute-done.3, f32[1,4,2,128,512]{4,3,2,1,0:T(8,128)} %bitcast.419, s32[]{:T(128)S(6)} %select_n.477), kind=kLoop, calls=%fused_computation.36 | loop fusion | flops 262144 | bytes 3145732 | tf_op jit(solution)/shard_map/add | solution.py:94
  87.2 2.8 %collective-permute-start.4 = (f32[1,1,256,512]{3,2,1,0:T(8,128)S(1)}, f32[1,1,256,512]{3,2,1,0:T(8,128)S(1)}, u32[]{:S(2)}, u32[]{:S(2)}) collective-permute-start(f32[1,1,256,512]{3,2,1,0:T(8,128)S(1)} %dynamic-slice_bitcast_fusion.1), channel_id=1, source_target_pairs={{0,16},{16,0},{4,20},{20,4},{8,24},{24,8},{12,28},{28,12},{1,17},{... | collective-permute-start | bytes 1572872 | tf_op jit(solution)/shard_map/ppermute | solution.py:26
  90.0 23.5 %collective-permute-done.4 = f32[1,1,256,512]{3,2,1,0:T(8,128)S(1)} collective-permute-done((f32[1,1,256,512]{3,2,1,0:T(8,128)S(1)}, f32[1,1,256,512]{3,2,1,0:T(8,128)S(1)}, u32[]{:S(2)}, u32[]{:S(2)}) %collective-permute-start.4) | collective-permute-done | bytes 524320 | tf_op jit(solution)/shard_map/ppermute | solution.py:26
  113.6 0.8 collective-permute-start.5
  114.4 0.7 fusion.77
  130.5 1.4 %collective-permute-done.6 = f32[1,128,384]{2,1,0:T(8,128)S(1)} collective-permute-done((f32[1,128,384]{2,1,0:T(8,128)S(1)}, f32[1,128,384]{2,1,0:T(8,128)S(1)}, u32[]{:S(2)}, u32[]{:S(2)}) %collective-permute-start.6) | collective-permute-done | bytes 196640 | tf_op jit(solution)/shard_map/ppermute | solution.py:127
  133.4 2.0 %copy.37 = f32[1,256,8,256]{3,2,1,0:T(8,128)} copy(f32[1,256,8,256]{1,3,2,0:T(8,128)S(1)} %broadcast_multiply_fusion) | data formatting | bytes 4194304 | tf_op jit(solution)/shard_map/mul | solution.py:142
  (216 shorter events, 24.1 us)
Async XLA Ops:
  2.8 5.7 %all-to-all-start = ((f32[1,1024,256]{2,0,1:T(1,128)}), f32[1,1024,256]{2,0,1:T(1,128)S(1)}, u32[]{:S(2)}, u32[]{:S(2)}) async-start(f32[1,1024,256]{2,0,1:T(1,128)} %copy.32), calls=%async_computation | async-start | bytes 2097152 | tf_op jit(solution)/shard_map/all_to_all | solution.py:105
  9.3 2.0 %copy-start.1 = (s32[3,12,2048]{2,1,0:T(8,128)S(1)}, s32[3,12,2048]{2,1,0:T(8,128)}, u32[]{:S(2)}) copy-start(s32[3,12,2048]{2,1,0:T(8,128)} %param.16) | copy-start | bytes 884740
  39.2 1.6 %collective-permute-start = (f32[1,1,128,512]{3,2,1,0:T(8,128)S(1)}, f32[1,1,128,512]{3,2,1,0:T(8,128)S(1)}, u32[]{:S(2)}, u32[]{:S(2)}) collective-permute-start(f32[1,1,128,512]{3,2,1,0:T(8,128)S(1)} %dynamic-slice_bitcast_fusion.4), channel_id=1, source_target_pairs={{0,4},{4,0},{8,12},{12,8},{16,20},{20,16},{24,28},{28,24},{1,5},{5... | collective-permute-start | bytes 786440 | tf_op jit(solution)/shard_map/ppermute | solution.py:26
  49.0 1.8 %copy-start.2 = (s32[3,1,2048]{2,1,0:T(1,128)S(1)}, s32[3,1,2048]{2,1,0:T(1,128)}, u32[]{:S(2)}) copy-start(s32[3,1,2048]{2,1,0:T(1,128)} %get-tuple-element.85) | copy-start | bytes 73732
  50.7 2.0 %collective-permute-start.1 = (f32[1,2,128,512]{3,2,1,0:T(8,128)S(1)}, f32[1,2,128,512]{3,2,1,0:T(8,128)S(1)}, u32[]{:S(2)}, u32[]{:S(2)}) collective-permute-start(f32[1,2,128,512]{3,2,1,0:T(8,128)S(1)} %dynamic-slice_bitcast_fusion.2), channel_id=1, source_target_pairs={{0,4},{4,0},{8,12},{12,8},{16,20},{20,16},{24,28},{28,24},{1,5},{5... | collective-permute-start | bytes 1572872 | tf_op jit(solution)/shard_map/ppermute | solution.py:26
  52.8 9.7 %collective-permute-start.2 = (f32[1,1,128,512]{3,2,1,0:T(8,128)S(1)}, f32[1,1,128,512]{3,2,1,0:T(8,128)S(1)}, u32[]{:S(2)}, u32[]{:S(2)}) collective-permute-start(f32[1,1,128,512]{3,2,1,0:T(8,128)S(1)} %constant_dynamic-slice_fusion.21), channel_id=1, source_target_pairs={{0,8},{8,0},{4,12},{12,4},{16,24},{24,16},{20,28},{28,20},{1,9},{9... | collective-permute-start | bytes 786440 | tf_op jit(solution)/shard_map/ppermute | solution.py:26
  81.5 1.3 copy-start
  82.9 2.7 %collective-permute-start.3 = (f32[1,4,128,512]{3,2,1,0:T(8,128)S(1)}, f32[1,4,128,512]{3,2,1,0:T(8,128)S(1)}, u32[]{:S(2)}, u32[]{:S(2)}) collective-permute-start(f32[1,4,128,512]{3,2,1,0:T(8,128)S(1)} %dynamic-slice_bitcast_fusion), channel_id=1, source_target_pairs={{0,4},{4,0},{8,12},{12,8},{16,20},{20,16},{24,28},{28,24},{1,5},{5... | collective-permute-start | bytes 3145736 | tf_op jit(solution)/shard_map/ppermute | solution.py:26
  87.1 27.3 %copy-start.3 = (s32[8]{0:T(128)S(1)}, s32[8]{0:T(128)}, u32[]{:S(2)}) copy-start(s32[8]{0:T(128)} %param.17) | copy-start | bytes 100
  87.2 26.3 %collective-permute-start.4 = (f32[1,1,256,512]{3,2,1,0:T(8,128)S(1)}, f32[1,1,256,512]{3,2,1,0:T(8,128)S(1)}, u32[]{:S(2)}, u32[]{:S(2)}) collective-permute-start(f32[1,1,256,512]{3,2,1,0:T(8,128)S(1)} %dynamic-slice_bitcast_fusion.1), channel_id=1, source_target_pairs={{0,16},{16,0},{4,20},{20,4},{8,24},{24,8},{12,28},{28,12},{1,17},{... | collective-permute-start | bytes 1572872 | tf_op jit(solution)/shard_map/ppermute | solution.py:26
  113.6 16.3 %collective-permute-start.5 = (f32[1,1,128,512]{3,2,1,0:T(8,128)S(1)}, f32[1,1,128,512]{3,2,1,0:T(8,128)S(1)}, u32[]{:S(2)}, u32[]{:S(2)}) collective-permute-start(f32[1,1,128,512]{3,2,1,0:T(8,128)S(1)} %dynamic-slice_bitcast_fusion.3), channel_id=1, source_target_pairs={{0,8},{8,0},{4,12},{12,4},{16,24},{24,16},{20,28},{28,20},{1,9},{9... | collective-permute-start | bytes 786440 | tf_op jit(solution)/shard_map/ppermute | solution.py:26
  130.4 1.5 %collective-permute-start.6 = (f32[1,128,384]{2,1,0:T(8,128)S(1)}, f32[1,128,384]{2,1,0:T(8,128)S(1)}, u32[]{:S(2)}, u32[]{:S(2)}) collective-permute-start(f32[1,128,384]{2,1,0:T(8,128)S(1)} %pad_dynamic-slice_fusion), channel_id=1, source_target_pairs={{0,4},{4,0},{1,5},{5,1},{2,6},{6,2},{3,7},{7,3},{8,12},{12,8},{9,1... | collective-permute-start | bytes 589832 | tf_op jit(solution)/shard_map/ppermute | solution.py:127

commit v5 on v3

--- a/solution.py
+++ b/solution.py
@@ -82,15 +82,13 @@
     partial_value = jnp.where(lower_hit[None, :, None], lower_rows, 0.0) + jnp.where(
         upper_hit[None, :, None], upper_rows, 0.0
     )
-    for bit_index in range(cross_step + 1):
-        blocks = partial_value.shape[1] // rows_held
-        paired = partial_value.reshape(beam_count, blocks // 2, 2, rows_held, columns)
-        chosen_bit = device_pos >> bit_index & 1
-        kept_rows = lax.dynamic_index_in_dim(paired, chosen_bit, 2, keepdims=False)
-        given_rows = lax.dynamic_index_in_dim(paired, 1 - chosen_bit, 2, keepdims=False)
-        partial_value = (kept_rows + swapped(given_rows, bit_index)).reshape(
-            beam_count, blocks // 2 * rows_held, columns
-        )
+    blocks = partial_value.reshape(beam_count, group_size, rows_held, columns)
+    total = lax.dynamic_index_in_dim(blocks, position, 1, keepdims=False)
+    for offset in range(1, group_size):
+        sent = lax.dynamic_index_in_dim(blocks, position ^ offset, 1, keepdims=False)
+        route = [(low, low ^ offset) for low in range(band_count())]
+        total = total + lax.ppermute(sent, BANDS, route)
+    partial_value = total
     return partial_value
 
 

time: 123 us -> 138 us (1.12)
  the two profiles are of different devices: /device:TPU:0 before, /device:TPU:19 now
where the time goes in v5:
time: 138 us
  local copies, waits for them, and re-layouts  52.6 us (38%)
  waiting for transfers between devices  39.3 us (28%)
  between operations  16.7 us (12%)
  other arithmetic  15.2 us (11%)
  starting transfers between devices  13.9 us (10%)
    ppermute x11, waiting for transfers between devices, merge_across(): total = total + lax.ppermute(sent, BANDS, route)  36.5 us
    slice x45, local copies, waits for them, and re-layouts, shift_rows(): result[..., step_size:]  11.8 us
    ppermute x11, starting transfers between devices, merge_across(): total = total + lax.ppermute(sent, BANDS, route)  8.58 us
    gather x3, local copies, waits for them, and re-layouts, merge_across(): jnp.take(current, jnp.clip(lower_local, 0, rows_held - 1), axis=1)  7.46 us
    gather x9, local copies, waits for them, and re-layouts, merge_bands(): picked = jnp.take(lower_flat, band_base + entries[0], axis=1)  7.02 us
    gather x9, local copies, waits for them, and re-layouts, merge_bands(): chosen = jnp.take(upper_flat, band_base + entries[1], axis=1)  7.02 us
    select_n x36, other arithmetic, shift_rows(): result = jnp.where(flag[None, :, None], moved, result)  6.33 us
    gather x3, local copies, waits for them, and re-layouts, merge_across(): jnp.take(current, jnp.clip(upper_local, 0, rows_held - 1), axis=1)  6.32 us
  transfers between devices with their start and end apart: 13, of which 8 were waited for; matrix products, arithmetic and copies ran while one was open for 2% of the time, Pallas kernels for 0%

profile of v5, /device:TPU:19, one launch (start us, length us, event | category | flops | bytes accessed | tf_op | source)
XLA Modules:
  0.0 137.8 jit_solution(5334310930647667821)
XLA Ops:
  0.0 2.8 %copy.38 = f32[1,1024,256]{2,0,1:T(1,128)} copy(bf16[1,1024,256]{2,1,0:T(8,128)(2,1)} %param.15) | data formatting | bytes 1572864 | tf_op jit(solution)/shard_map/convert_element_type | solution.py:100
  2.8 4.2 %all-to-all-start = ((f32[1,1024,256]{2,0,1:T(1,128)}), f32[1,1024,256]{2,0,1:T(1,128)S(1)}, u32[]{:S(2)}, u32[]{:S(2)}) async-start(f32[1,1024,256]{2,0,1:T(1,128)} %copy.38), calls=%async_computation | async-start | bytes 2097152 | tf_op jit(solution)/shard_map/all_to_all | solution.py:100
  7.1 1.7 %all-to-all-done = f32[1,1024,256]{2,0,1:T(1,128)S(1)} async-done(((f32[1,1024,256]{2,0,1:T(1,128)}), f32[1,1024,256]{2,0,1:T(1,128)S(1)}, u32[]{:S(2)}, u32[]{:S(2)}) %all-to-all-start) | async-done | bytes 1048608 | tf_op jit(solution)/shard_map/all_to_all | solution.py:100
  8.8 0.8 copy.54
  9.6 0.8 broadcast_in_dim.430
  11.9 1.0 gather_fusion
  12.9 1.0 gather_fusion.1
  14.7 0.8 gather_fusion.2
  15.5 0.8 gather_fusion.3
  17.0 0.8 gather_fusion.4
  17.8 0.8 gather_fusion.5
  19.0 0.8 gather_fusion.7
  20.1 0.8 gather_fusion.6
  21.1 0.8 gather_fusion.9
  22.4 0.8 gather_fusion.8
  23.4 0.8 gather_fusion.11
  24.9 0.8 gather_fusion.10
  25.8 0.8 gather_fusion.13
  27.5 0.8 gather_fusion.12
  28.4 0.8 gather_fusion.15
  30.4 0.8 gather_fusion.14
  31.3 0.8 gather_fusion.17
  33.5 0.8 gather_fusion.16
  34.4 1.0 gather_fusion.19
  37.7 1.0 gather_fusion.18
  39.6 0.9 collective-permute-done
  40.6 1.8 %gather_fusion.21 = f32[512,512]{1,0:T(8,128)S(1)} fusion(f32[128,512]{1,0:T(8,128)S(1)} %fusion.19, s32[1024]{0:T(1024)S(1)} %pad_clamp_fusion), kind=kCustom, calls=%fused_computation.22.clone | custom fusion | bytes 2099200 | tf_op jit(solution)/shard_map/jit(_take)/gather | solution.py:80
  46.2 0.9 slice.601
  47.2 1.6 %gather_fusion.20 = f32[512,512]{1,0:T(8,128)S(1)} fusion(f32[128,512]{1,0:T(8,128)S(1)} %fusion.19, s32[1024]{0:T(1024)S(1)} %pad_clamp_fusion.1), kind=kCustom, calls=%fused_computation.4.clone | custom fusion | bytes 2099200 | tf_op jit(solution)/shard_map/jit(_take)/gather | solution.py:77
  48.8 1.6 %fusion.3 = f32[1,512,512]{2,1,0:T(8,128)S(1)} fusion(f32[512,512]{1,0:T(8,128)S(1)} %gather_fusion.20, f32[1,512,512]{2,1,0:T(8,128)S(1)} %pad_select_fusion.8, f32[1,512,384]{2,1,0:T(8,128)} %slice.601, pred[512]{0:T(512)(128)(4,1)S(1)} %get-tuple-element.203, pred[512]{0:T(512)(128)(4,1)S(1)} %get-tuple-element.26, ...), kind=kLoop, calls=%fused_computation.39 | loop fusion | flops 1310720 | bytes 3934208 | tf_op jit(solution)/shard_map/add | solution.py:82
  50.9 1.3 collective-permute-start.2
  53.0 5.7 %collective-permute-done.2 = f32[1,128,512]{2,1,0:T(8,128)S(1)} collective-permute-done((f32[1,128,512]{2,1,0:T(8,128)S(1)}, f32[1,128,512]{2,1,0:T(8,128)S(1)}, u32[]{:S(2)}, u32[]{:S(2)}) %collective-permute-start.2) | collective-permute-done | bytes 262176 | tf_op jit(solution)/shard_map/ppermute | solution.py:90
  58.6 5.9 %collective-permute-done.3 = f32[1,128,512]{2,1,0:T(8,128)S(1)} collective-permute-done((f32[1,128,512]{2,1,0:T(8,128)S(1)}, f32[1,128,512]{2,1,0:T(8,128)S(1)}, u32[]{:S(2)}, u32[]{:S(2)}) %collective-permute-start.3) | collective-permute-done | bytes 262176 | tf_op jit(solution)/shard_map/ppermute | solution.py:90
  64.6 3.5 %gather_fusion.23 = f32[1024,512]{1,0:T(8,128)S(1)} fusion(f32[128,512]{1,0:T(8,128)S(1)} %fusion.18, s32[1024]{0:T(1024)S(1)} %get-tuple-element.201), kind=kCustom, calls=%fused_computation.23.clone | custom fusion | bytes 4198400 | tf_op jit(solution)/shard_map/jit(_take)/gather | solution.py:80
  69.0 1.0 pad_select_fusion.7
  75.9 4.9 %gather_fusion.22 = f32[1024,512]{1,0:T(8,128)} fusion(f32[128,512]{1,0:T(8,128)S(1)} %fusion.18, s32[1024]{0:T(1024)S(1)} %get-tuple-element.200), kind=kCustom, calls=%fused_computation.5.clone | custom fusion | bytes 4198400 | tf_op jit(solution)/shard_map/jit(_take)/gather | solution.py:77
  80.7 2.9 %fusion.1 = f32[1,1024,512]{2,1,0:T(8,128)S(1)} fusion(f32[1024,512]{1,0:T(8,128)} %gather_fusion.22, f32[1,1024,512]{2,1,0:T(8,128)S(1)} %pad_select_fusion, f32[1,1024,256]{2,1,0:T(8,128)S(1)} %slice.610, pred[1024]{0:T(1024)(128)(4,1)S(1)} %get-tuple-element.199, pred[1024]{0:T(1024)(128)(4,1)S(1)} %get-tuple-element.20, ...), kind=kLoop, calls=%fused_computation.27 | loop fusion | flops 2621440 | bytes 7344128 | tf_op jit(solution)/shard_map/add | solution.py:82
  83.9 0.8 copy.47
  85.6 1.1 collective-permute-start.5
  86.8 0.7 collective-permute-start.6
  87.7 3.3 %collective-permute-start.7 = (f32[1,128,512]{1,2,0:T(8,128)S(1)}, f32[1,128,512]{1,2,0:T(8,128)S(1)}, u32[]{:S(2)}, u32[]{:S(2)}) collective-permute-start(f32[1,128,512]{1,2,0:T(8,128)S(1)} %bitcast.438), channel_id=1, source_target_pairs={{0,16},{4,20},{8,24},{12,28},{16,0},{20,4},{24,8},{28,12},{1,17},{... | collective-permute-start | bytes 786440 | tf_op jit(solution)/shard_map/ppermute | solution.py:90
  91.0 0.8 copy.45
  91.9 7.5 %collective-permute-done.10 = f32[1,128,512]{1,2,0:T(8,128)S(1)} collective-permute-done((f32[1,128,512]{1,2,0:T(8,128)}, f32[1,128,512]{1,2,0:T(8,128)S(1)}, u32[]{:S(2)}, u32[]{:S(2)}) %collective-permute-start.10) | collective-permute-done | bytes 262176 | tf_op jit(solution)/shard_map/ppermute | solution.py:90
  115.5 9.0 %collective-permute-done.8 = f32[1,128,512]{1,2,0:T(8,128)S(1)} collective-permute-done((f32[1,128,512]{1,2,0:T(8,128)}, f32[1,128,512]{1,2,0:T(8,128)S(1)}, u32[]{:S(2)}, u32[]{:S(2)}) %collective-permute-start.8) | collective-permute-done | bytes 262176 | tf_op jit(solution)/shard_map/ppermute | solution.py:90
  124.4 7.5 %collective-permute-done.9 = f32[1,128,512]{1,2,0:T(8,128)S(1)} collective-permute-done((f32[1,128,512]{1,2,0:T(8,128)S(1)}, f32[1,128,512]{1,2,0:T(8,128)S(1)}, u32[]{:S(2)}, u32[]{:S(2)}) %collective-permute-start.9) | collective-permute-done | bytes 262176 | tf_op jit(solution)/shard_map/ppermute | solution.py:90
  132.3 1.1 collective-permute-start.11
  133.3 1.1 collective-permute-done.11
  135.8 2.0 %copy.50 = f32[1,256,8,256]{3,2,1,0:T(8,128)} copy(f32[1,256,8,256]{1,3,2,0:T(8,128)S(1)} %broadcast_multiply_fusion) | data formatting | bytes 4194304 | tf_op jit(solution)/shard_map/mul | solution.py:137
  (227 shorter events, 27.6 us)
Async XLA Ops:
  2.8 6.0 %all-to-all-start = ((f32[1,1024,256]{2,0,1:T(1,128)}), f32[1,1024,256]{2,0,1:T(1,128)S(1)}, u32[]{:S(2)}, u32[]{:S(2)}) async-start(f32[1,1024,256]{2,0,1:T(1,128)} %copy.38), calls=%async_computation | async-start | bytes 2097152 | tf_op jit(solution)/shard_map/all_to_all | solution.py:100
  9.6 2.0 %copy-start = (s32[3,12,2048]{2,1,0:T(8,128)S(1)}, s32[3,12,2048]{2,1,0:T(8,128)}, u32[]{:S(2)}) copy-start(s32[3,12,2048]{2,1,0:T(8,128)} %param.16) | copy-start | bytes 884740
  11.8 27.7 %copy-start.1 = (s32[3,1,2048]{2,1,0:T(1,128)}, s32[3,1,2048]{2,1,0:T(1,128)S(1)}, u32[]{:S(2)}) copy-start(s32[3,1,2048]{2,1,0:T(1,128)S(1)} %get-tuple-element.96) | copy-start | bytes 73732
  39.0 1.6 %collective-permute-start = (f32[1,128,512]{2,1,0:T(8,128)S(1)}, f32[1,128,512]{2,1,0:T(8,128)S(1)}, u32[]{:S(2)}, u32[]{:S(2)}) collective-permute-start(f32[1,128,512]{2,1,0:T(8,128)S(1)} %dynamic-slice_bitcast_fusion.3), channel_id=1, source_target_pairs={{0,4},{4,0},{8,12},{12,8},{16,20},{20,16},{24,28},{28,24},{1,5},{5... | collective-permute-start | bytes 786440 | tf_op jit(solution)/shard_map/ppermute | solution.py:90
  48.8 4.0 %copy-start.2 = (s32[3,1,2048]{2,1,0:T(1,128)S(1)}, s32[3,1,2048]{2,1,0:T(1,128)}, u32[]{:S(2)}) copy-start(s32[3,1,2048]{2,1,0:T(1,128)} %copy-done.1) | copy-start | bytes 73732
  50.5 2.5 %collective-permute-start.1 = (f32[1,128,512]{2,1,0:T(8,128)S(1)}, f32[1,128,512]{2,1,0:T(8,128)S(1)}, u32[]{:S(2)}, u32[]{:S(2)}) collective-permute-start(f32[1,128,512]{2,1,0:T(8,128)S(1)} %get-tuple-element.91), channel_id=1, source_target_pairs={{0,4},{4,0},{8,12},{12,8},{16,20},{20,16},{24,28},{28,24},{1,5},{5... | collective-permute-start | bytes 786440 | tf_op jit(solution)/shard_map/ppermute | solution.py:90
  50.9 7.7 %collective-permute-start.2 = (f32[1,128,512]{2,1,0:T(8,128)S(1)}, f32[1,128,512]{2,1,0:T(8,128)S(1)}, u32[]{:S(2)}, u32[]{:S(2)}) collective-permute-start(f32[1,128,512]{2,1,0:T(8,128)S(1)} %get-tuple-element.93), channel_id=1, source_target_pairs={{0,8},{4,12},{8,0},{12,4},{16,24},{20,28},{24,16},{28,20},{1,9},{5... | collective-permute-start | bytes 786440 | tf_op jit(solution)/shard_map/ppermute | solution.py:90
  52.2 12.4 %collective-permute-start.3 = (f32[1,128,512]{2,1,0:T(8,128)S(1)}, f32[1,128,512]{2,1,0:T(8,128)S(1)}, u32[]{:S(2)}, u32[]{:S(2)}) collective-permute-start(f32[1,128,512]{2,1,0:T(8,128)S(1)} %get-tuple-element.92), channel_id=1, source_target_pairs={{0,12},{4,8},{8,4},{12,0},{16,28},{20,24},{24,20},{28,16},{1,13},{... | collective-permute-start | bytes 786440 | tf_op jit(solution)/shard_map/ppermute | solution.py:90
  83.8 15.8 %copy-start.3 = (s32[8]{0:T(128)S(1)}, s32[8]{0:T(128)}, u32[]{:S(2)}) copy-start(s32[8]{0:T(128)} %param.17) | copy-start | bytes 100
  84.7 14.7 %collective-permute-start.10 = (f32[1,128,512]{1,2,0:T(8,128)}, f32[1,128,512]{1,2,0:T(8,128)S(1)}, u32[]{:S(2)}, u32[]{:S(2)}) collective-permute-start(f32[1,128,512]{1,2,0:T(8,128)} %bitcast.124), channel_id=1, source_target_pairs={{0,28},{4,24},{8,20},{12,16},{16,12},{20,8},{24,4},{28,0},{1,29},{... | collective-permute-start | bytes 786440 | tf_op jit(solution)/shard_map/ppermute | solution.py:90
  85.0 14.5 %collective-permute-start.4 = (f32[1,128,512]{1,2,0:T(8,128)S(1)}, f32[1,128,512]{1,2,0:T(8,128)S(1)}, u32[]{:S(2)}, u32[]{:S(2)}) collective-permute-start(f32[1,128,512]{1,2,0:T(8,128)S(1)} %bitcast.440), channel_id=1, source_target_pairs={{0,4},{4,0},{8,12},{12,8},{16,20},{20,16},{24,28},{28,24},{1,5},{5... | collective-permute-start | bytes 786440 | tf_op jit(solution)/shard_map/ppermute | solution.py:90
  85.6 29.9 %collective-permute-start.5 = (f32[1,128,512]{1,2,0:T(8,128)S(1)}, f32[1,128,512]{1,2,0:T(8,128)S(1)}, u32[]{:S(2)}, u32[]{:S(2)}) collective-permute-start(f32[1,128,512]{1,2,0:T(8,128)S(1)} %bitcast.436), channel_id=1, source_target_pairs={{0,8},{4,12},{8,0},{12,4},{16,24},{20,28},{24,16},{28,20},{1,9},{5... | collective-permute-start | bytes 786440 | tf_op jit(solution)/shard_map/ppermute | solution.py:90
  86.8 28.6 %collective-permute-start.6 = (f32[1,128,512]{1,2,0:T(8,128)S(1)}, f32[1,128,512]{1,2,0:T(8,128)S(1)}, u32[]{:S(2)}, u32[]{:S(2)}) collective-permute-start(f32[1,128,512]{1,2,0:T(8,128)S(1)} %bitcast.437), channel_id=1, source_target_pairs={{0,12},{4,8},{8,4},{12,0},{16,28},{20,24},{24,20},{28,16},{1,13},{... | collective-permute-start | bytes 786440 | tf_op jit(solution)/shard_map/ppermute | solution.py:90
  87.7 27.8 %collective-permute-start.7 = (f32[1,128,512]{1,2,0:T(8,128)S(1)}, f32[1,128,512]{1,2,0:T(8,128)S(1)}, u32[]{:S(2)}, u32[]{:S(2)}) collective-permute-start(f32[1,128,512]{1,2,0:T(8,128)S(1)} %bitcast.438), channel_id=1, source_target_pairs={{0,16},{4,20},{8,24},{12,28},{16,0},{20,4},{24,8},{28,12},{1,17},{... | collective-permute-start | bytes 786440 | tf_op jit(solution)/shard_map/ppermute | solution.py:90
  99.4 25.0 %collective-permute-start.8 = (f32[1,128,512]{1,2,0:T(8,128)}, f32[1,128,512]{1,2,0:T(8,128)S(1)}, u32[]{:S(2)}, u32[]{:S(2)}) collective-permute-start(f32[1,128,512]{1,2,0:T(8,128)} %bitcast.122), channel_id=1, source_target_pairs={{0,20},{4,16},{8,28},{12,24},{16,4},{20,0},{24,12},{28,8},{1,21},{... | collective-permute-start | bytes 786440 | tf_op jit(solution)/shard_map/ppermute | solution.py:90
  99.4 32.6 %collective-permute-start.9 = (f32[1,128,512]{1,2,0:T(8,128)S(1)}, f32[1,128,512]{1,2,0:T(8,128)S(1)}, u32[]{:S(2)}, u32[]{:S(2)}) collective-permute-start(f32[1,128,512]{1,2,0:T(8,128)S(1)} %bitcast.439), channel_id=1, source_target_pairs={{0,24},{4,28},{8,16},{12,20},{16,8},{20,12},{24,0},{28,4},{1,25},{... | collective-permute-start | bytes 786440 | tf_op jit(solution)/shard_map/ppermute | solution.py:90
  132.3 2.1 %collective-permute-start.11 = (f32[1,128,384]{1,2,0:T(8,128)S(1)}, f32[1,128,384]{1,2,0:T(8,128)S(1)}, u32[]{:S(2)}, u32[]{:S(2)}) collective-permute-start(f32[1,128,384]{1,2,0:T(8,128)S(1)} %pad_dynamic-slice_fusion), channel_id=1, source_target_pairs={{0,4},{4,0},{1,5},{5,1},{2,6},{6,2},{3,7},{7,3},{8,12},{12,8},{9,1... | collective-permute-start | bytes 589832 | tf_op jit(solution)/shard_map/ppermute | solution.py:122
